TPU v7x, 32 devices: a whole 2x2x4 slice. The times are simulated.
32 devices in a mesh: fsdp: 8 (over z, x), rep: 4 (over y, core).
Axes of the slice: x: 2, y: 2, z: 4, core: 2. Of those that a mesh axis runs over, the one named last changes fastest.
Arguments:
- latents: float32 [256, 256, 384], P(('fsdp', 'rep')), may hold values from -6 to 6
- condition: float32 [256, 384], P(('fsdp', 'rep')), may hold values from -6 to 6
- cotangent: float32 [256, 256, 384], P(('fsdp', 'rep')), may hold values from -6 to 6
- w_ada: bfloat16 [2, 384, 2304], P(None, 'fsdp'), may hold values from -0.3125 to 0.3125
- b_ada: bfloat16 [2, 2304], P(None, 'fsdp'), may hold values from -3 to 3
- w_qkv: bfloat16 [2, 384, 1152], P(None, 'fsdp'), may hold values from -0.3125 to 0.3125
- qv_bias: bfloat16 [2, 768], P(None, 'fsdp'), may hold values from -3 to 3
- w_out: bfloat16 [2, 384, 384], P(None, 'fsdp'), may hold values from -1.25 to 1.25
- b_out: bfloat16 [2, 384], P(None, 'fsdp'), may hold values from -3 to 3
- w_up: bfloat16 [2, 384, 1536], P(None, 'fsdp'), may hold values from -0.3125 to 0.3125
- b_up: bfloat16 [2, 1536], P(None, 'fsdp'), may hold values from -3 to 3
- w_down: bfloat16 [2, 1536, 384], P(None, 'fsdp'), may hold values from -0.15625 to 0.15625
- b_down: bfloat16 [2, 384], P(None, 'fsdp'), may hold values from -3 to 3
Outputs:
- output: float32 [256, 256, 384], P(('fsdp', 'rep'))
- grad_latents: float32 [256, 256, 384], P(('fsdp', 'rep'))
- grad_condition: float32 [256, 384], P(('fsdp', 'rep'))
- grad_w_ada: float32 [2, 384, 2304], P(None, 'fsdp')
- grad_b_ada: float32 [2, 2304], P(None, 'fsdp')
- grad_w_qkv: float32 [2, 384, 1152], P(None, 'fsdp')
- grad_qv_bias: float32 [2, 768], P(None, 'fsdp')
- grad_w_out: float32 [2, 384, 384], P(None, 'fsdp')
- grad_b_out: float32 [2, 384], P(None, 'fsdp')
- grad_w_up: float32 [2, 384, 1536], P(None, 'fsdp')
- grad_b_up: float32 [2, 1536], P(None, 'fsdp')
- grad_w_down: float32 [2, 1536, 384], P(None, 'fsdp')
- grad_b_down: float32 [2, 384], P(None, 'fsdp')
All inputs are finite; a program needn't handle non-finite values.
Results may differ from a plain program's by a relative error of at most 0.029.
The roundings to bfloat16 on the way count: a program that leaves them out, or rounds other values in their place, can miss the bound.
Values may be sent and summed in bfloat16 or wider, within the bound.
No kernel may reach another device: no remote copies, remote signals or barrier semaphores. Data moves between devices by JAX's collectives and lax.ppermute only.
A program may use at most 320 MiB of HBM per device.

v0:
```python
import jax
import jax.numpy as jnp
from jax import lax
from jax.sharding import PartitionSpec as P

LAYERS = 2


GELU_C = 0.7978845608028654
GELU_A = 0.044715
EPS = 1e-06


def as_sent(shard):

    def short(part):
        return part.astype(jnp.bfloat16) if part.dtype == jnp.float32 else part

    return jax.tree.map(short, shard)


def pair_product(form, left, right):
    return jnp.einsum(form, left, right, preferred_element_type=jnp.float32)


def matmul(inputs, weight):
    flattened = inputs.reshape(-1, inputs.shape[-1])
    result = jnp.dot(flattened, weight, preferred_element_type=jnp.float32)
    return result.reshape(inputs.shape[:-1] + (weight.shape[-1],))


def matmul_back(grads, weight):
    flattened = grads.reshape(-1, grads.shape[-1])
    result = lax.dot_general(
        flattened, weight, (((1,), (1,)), ((), ())), preferred_element_type=jnp.float32
    )
    return result.reshape(grads.shape[:-1] + (weight.shape[0],))


def outer_sum(left, right):
    return lax.dot_general(
        left.reshape(-1, left.shape[-1]),
        right.reshape(-1, right.shape[-1]),
        (((0,), (0,)), ((), ())),
        preferred_element_type=jnp.float32,
    )


def norm_rows(stream):
    centered = stream - jnp.mean(stream, axis=-1, keepdims=True)
    inverse = lax.rsqrt(jnp.mean(centered * centered, axis=-1, keepdims=True) + EPS)
    return (centered * inverse, inverse)


def norm_back(grad_normed, normed, inverse):
    return inverse * (
        grad_normed
        - jnp.mean(grad_normed, axis=-1, keepdims=True)
        - normed * jnp.mean(grad_normed * normed, axis=-1, keepdims=True)
    )


def gelu_parts(pre_act):
    tanh_part = jnp.tanh(GELU_C * (pre_act + GELU_A * pre_act * pre_act * pre_act))
    value_part = 0.5 * pre_act * (1.0 + tanh_part)
    slope_part = 0.5 * (1.0 + tanh_part) + 0.5 * pre_act * (
        1.0 - tanh_part * tanh_part
    ) * GELU_C * (1.0 + 3.0 * GELU_A * pre_act * pre_act)
    return (value_part, slope_part)


def forward_pieces(stream, cond_rows, params):
    w_ada, b_ada, w_qkv, qv_bias, w_out, b_out, w_up, b_up, w_down, b_down = params
    model_width = stream.shape[-1]
    head_count = model_width // 64
    silu_cond = jax.nn.silu(cond_rows).astype(jnp.bfloat16)
    modulation = jnp.dot(silu_cond, w_ada, preferred_element_type=jnp.float32) + b_ada.astype(
        jnp.float32
    )
    pieces = [modulation[:, None, i * model_width : (i + 1) * model_width] for i in range(6)]
    shift1, scale1, gate1, shift2, scale2, gate2 = pieces
    normed1, inverse1 = norm_rows(stream)
    attn_in = (normed1 * (1.0 + scale1) + shift1).astype(jnp.bfloat16)
    bias_query = qv_bias[:model_width].astype(jnp.float32)
    bias_value = qv_bias[model_width:].astype(jnp.float32)
    full_bias = jnp.concatenate([bias_query, jnp.zeros_like(bias_query), bias_value])
    projected = (matmul(attn_in, w_qkv) + full_bias).astype(jnp.bfloat16)
    head_shape = stream.shape[:2] + (head_count, 64)
    query = projected[..., :model_width].reshape(head_shape)
    key_heads = projected[..., model_width : 2 * model_width].reshape(head_shape)
    value_heads = projected[..., 2 * model_width :].reshape(head_shape)
    scores = pair_product("bqhe,bkhe->bhqk", query, key_heads) * 0.125
    log_total = jax.nn.logsumexp(scores, axis=-1, keepdims=True)
    attention = jnp.exp(scores - log_total)
    attention_b = attention.astype(jnp.bfloat16)
    attended = (
        pair_product("bhqk,bkhe->bqhe", attention_b, value_heads)
        .astype(jnp.bfloat16)
        .reshape(stream.shape)
    )
    branch = matmul(attended, w_out) + b_out.astype(jnp.float32)
    middle = stream + gate1 * branch
    normed2, inverse2 = norm_rows(middle)
    mlp_in = (normed2 * (1.0 + scale2) + shift2).astype(jnp.bfloat16)
    hidden_pre = matmul(mlp_in, w_up) + b_up.astype(jnp.float32)
    activated_f, slope = gelu_parts(hidden_pre)
    activated = activated_f.astype(jnp.bfloat16)
    mlp_out = matmul(activated, w_down) + b_down.astype(jnp.float32)
    result = middle + gate2 * mlp_out
    saved = (
        silu_cond,
        pieces,
        normed1,
        inverse1,
        attn_in,
        query,
        key_heads,
        value_heads,
        attention,
        attention_b,
        attended,
        branch,
        normed2,
        inverse2,
        mlp_in,
        slope,
        activated,
        mlp_out,
    )
    return (result, saved)


def layer_forward(stream, cond_rows, params):
    return forward_pieces(stream, cond_rows, params)[0]


def layer_grads(stream, cond_rows, params, grad_result):
    w_ada, b_ada, w_qkv, qv_bias, w_out, b_out, w_up, b_up, w_down, b_down = params
    result, saved = forward_pieces(stream, cond_rows, params)
    (
        silu_cond,
        pieces,
        normed1,
        inverse1,
        attn_in,
        query,
        key_heads,
        value_heads,
        attention,
        attention_b,
        attended,
        branch,
        normed2,
        inverse2,
        mlp_in,
        slope,
        activated,
        mlp_out,
    ) = saved
    shift1, scale1, gate1, shift2, scale2, gate2 = pieces
    grad_z = gate2 * grad_result
    grad_z_b = grad_z.astype(jnp.bfloat16)
    grad_gate2 = jnp.sum(grad_result * mlp_out, axis=1)
    grad_b_down = jnp.sum(grad_z, axis=(0, 1))
    grad_w_down = outer_sum(activated, grad_z_b)
    grad_pre = matmul_back(grad_z_b, w_down) * slope
    grad_pre_b = grad_pre.astype(jnp.bfloat16)
    grad_b_up = jnp.sum(grad_pre, axis=(0, 1))
    grad_w_up = outer_sum(mlp_in, grad_pre_b)
    grad_mlp_in = matmul_back(grad_pre_b, w_up)
    grad_scale2 = jnp.sum(grad_mlp_in * normed2, axis=1)
    grad_shift2 = jnp.sum(grad_mlp_in, axis=1)
    grad_middle = grad_result + norm_back(grad_mlp_in * (1.0 + scale2), normed2, inverse2)
    grad_branch = gate1 * grad_middle
    grad_branch_b = grad_branch.astype(jnp.bfloat16)
    grad_gate1 = jnp.sum(grad_middle * branch, axis=1)
    grad_b_out = jnp.sum(grad_branch, axis=(0, 1))
    grad_w_out = outer_sum(attended, grad_branch_b)
    grad_attended = matmul_back(grad_branch_b, w_out).astype(jnp.bfloat16).reshape(query.shape)
    grad_value = pair_product("bhqk,bqhe->bkhe", attention_b, grad_attended)
    grad_probs = pair_product("bqhe,bkhe->bhqk", grad_attended, value_heads)
    row_dot = jnp.sum(attention * grad_probs, axis=-1, keepdims=True)
    grad_scores = (attention * (grad_probs - row_dot) * 0.125).astype(jnp.bfloat16)
    grad_query = pair_product("bhqk,bkhe->bqhe", grad_scores, key_heads)
    grad_key = pair_product("bhqk,bqhe->bkhe", grad_scores, query)
    flat_shape = stream.shape
    grad_proj = jnp.concatenate(
        [
            grad_query.reshape(flat_shape),
            grad_key.reshape(flat_shape),
            grad_value.reshape(flat_shape),
        ],
        axis=-1,
    )
    grad_proj_b = grad_proj.astype(jnp.bfloat16)
    grad_qv_bias = jnp.concatenate(
        [
            jnp.sum(grad_query.reshape(flat_shape), axis=(0, 1)),
            jnp.sum(grad_value.reshape(flat_shape), axis=(0, 1)),
        ]
    )
    grad_w_qkv = outer_sum(attn_in, grad_proj_b)
    grad_attn_in = matmul_back(grad_proj_b, w_qkv)
    grad_scale1 = jnp.sum(grad_attn_in * normed1, axis=1)
    grad_shift1 = jnp.sum(grad_attn_in, axis=1)
    grad_stream = grad_middle + norm_back(grad_attn_in * (1.0 + scale1), normed1, inverse1)
    grad_mod = jnp.concatenate(
        [grad_shift1, grad_scale1, grad_gate1, grad_shift2, grad_scale2, grad_gate2], axis=-1
    )
    grad_w_ada = jnp.dot(silu_cond.astype(jnp.float32).T, grad_mod, precision=lax.Precision.HIGHEST)
    grad_b_ada = jnp.sum(grad_mod, axis=0)
    grad_silu = jnp.dot(grad_mod, w_ada.astype(jnp.float32).T, precision=lax.Precision.HIGHEST)
    sigmoid_c = jax.nn.sigmoid(cond_rows)
    grad_cond = grad_silu * sigmoid_c * (1.0 + cond_rows * (1.0 - sigmoid_c))
    gradients = (
        grad_w_ada,
        grad_b_ada,
        grad_w_qkv,
        grad_qv_bias,
        grad_w_out,
        grad_b_out,
        grad_w_up,
        grad_b_up,
        grad_w_down,
        grad_b_down,
    )
    return (grad_stream, grad_cond, gradients)


def body(
    latents,
    condition,
    cotangent,
    w_ada,
    b_ada,
    w_qkv,
    qv_bias,
    w_out,
    b_out,
    w_up,
    b_up,
    w_down,
    b_down,
):
    stacked = (w_ada, b_ada, w_qkv, qv_bias, w_out, b_out, w_up, b_up, w_down, b_down)
    inputs = []
    kept_weights = []
    stream = latents
    for layer_index in range(LAYERS):
        owned_rows = tuple((weight[layer_index] for weight in stacked))
        params = jax.tree.map(
            lambda part, own: part.astype(own.dtype),
            lax.all_gather(as_sent(owned_rows), "fsdp", axis=0, tiled=True),
            owned_rows,
        )
        kept_weights.append(params)
        inputs.append(stream)
        stream = layer_forward(stream, condition, params)
    grad_stream = cotangent
    grad_cond = jnp.zeros(condition.shape, jnp.float32)
    shards = [None] * LAYERS
    for layer_index in reversed(range(LAYERS)):
        owned_rows = tuple((weight[layer_index] for weight in stacked))
        params = jax.tree.map(
            lambda part, own: part.astype(own.dtype),
            lax.all_gather(as_sent(owned_rows), "fsdp", axis=0, tiled=True),
            owned_rows,
        )
        grad_stream, cond_part, gradients = layer_grads(
            inputs[layer_index], condition, params, grad_stream
        )
        grad_cond = grad_cond + cond_part
        owned_sums = (
            lax.psum_scatter(
                gradients[0].astype(jnp.bfloat16), "fsdp", scatter_dimension=0, tiled=True
            ).astype(jnp.float32),
            lax.psum_scatter(
                gradients[1].astype(jnp.bfloat16), "fsdp", scatter_dimension=0, tiled=True
            ).astype(jnp.float32),
            lax.psum_scatter(
                gradients[2].astype(jnp.bfloat16), "fsdp", scatter_dimension=0, tiled=True
            ).astype(jnp.float32),
            lax.psum_scatter(
                gradients[3].astype(jnp.bfloat16), "fsdp", scatter_dimension=0, tiled=True
            ).astype(jnp.float32),
            lax.psum_scatter(
                gradients[4].astype(jnp.bfloat16), "fsdp", scatter_dimension=0, tiled=True
            ).astype(jnp.float32),
            lax.psum_scatter(
                gradients[5].astype(jnp.bfloat16), "fsdp", scatter_dimension=0, tiled=True
            ).astype(jnp.float32),
            lax.psum_scatter(
                gradients[6].astype(jnp.bfloat16), "fsdp", scatter_dimension=0, tiled=True
            ).astype(jnp.float32),
            lax.psum_scatter(
                gradients[7].astype(jnp.bfloat16), "fsdp", scatter_dimension=0, tiled=True
            ).astype(jnp.float32),
            lax.psum_scatter(
                gradients[8].astype(jnp.bfloat16), "fsdp", scatter_dimension=0, tiled=True
            ).astype(jnp.float32),
            lax.psum_scatter(
                gradients[9].astype(jnp.bfloat16), "fsdp", scatter_dimension=0, tiled=True
            ).astype(jnp.float32),
        )
        owned_sums = (
            lax.psum(owned_sums[0].astype(jnp.bfloat16), "rep").astype(jnp.float32),
            lax.psum(owned_sums[1].astype(jnp.bfloat16), "rep").astype(jnp.float32),
            lax.psum(owned_sums[2].astype(jnp.bfloat16), "rep").astype(jnp.float32),
            lax.psum(owned_sums[3].astype(jnp.bfloat16), "rep").astype(jnp.float32),
            lax.psum(owned_sums[4].astype(jnp.bfloat16), "rep").astype(jnp.float32),
            lax.psum(owned_sums[5].astype(jnp.bfloat16), "rep").astype(jnp.float32),
            lax.psum(owned_sums[6].astype(jnp.bfloat16), "rep").astype(jnp.float32),
            lax.psum(owned_sums[7].astype(jnp.bfloat16), "rep").astype(jnp.float32),
            lax.psum(owned_sums[8].astype(jnp.bfloat16), "rep").astype(jnp.float32),
            lax.psum(owned_sums[9].astype(jnp.bfloat16), "rep").astype(jnp.float32),
        )
        shards[layer_index] = owned_sums
    stacked_grads = tuple((jnp.stack([shards[j][i] for j in range(LAYERS)]) for i in range(10)))
    return (stream, grad_stream, grad_cond) + stacked_grads


def solution(mesh):
    in_specs = (
        P(("fsdp", "rep"), None, None),
        P(("fsdp", "rep"), None),
        P(("fsdp", "rep"), None, None),
        P(None, "fsdp", None),
        P(None, "fsdp"),
        P(None, "fsdp", None),
        P(None, "fsdp"),
        P(None, "fsdp", None),
        P(None, "fsdp"),
        P(None, "fsdp", None),
        P(None, "fsdp"),
        P(None, "fsdp", None),
        P(None, "fsdp"),
    )
    out_specs = (
        P(("fsdp", "rep"), None, None),
        P(("fsdp", "rep"), None, None),
        P(("fsdp", "rep"), None),
        P(None, "fsdp", None),
        P(None, "fsdp"),
        P(None, "fsdp", None),
        P(None, "fsdp"),
        P(None, "fsdp", None),
        P(None, "fsdp"),
        P(None, "fsdp", None),
        P(None, "fsdp"),
        P(None, "fsdp", None),
        P(None, "fsdp"),
    )
    return jax.shard_map(body, mesh=mesh, in_specs=in_specs, out_specs=out_specs, check_vma=False)
```

profile of v0, /device:TPU:0, one launch (start us, length us, event | category | flops | bytes accessed | tf_op | source)
XLA Modules:
  0.0 1180.2 jit_solution(6326753263943865538)
XLA Ops:
  20.5 39.6 %all-reduce.21 = (bf16[768]{0:T(1024)(128)(2,1)S(1)}, bf16[2304]{0:T(1024)(128)(2,1)S(1)}, bf16[384]{0:T(512)(128)(2,1)S(1)}, bf16[1536]{0:T(1024)(128)(2,1)S(1)...) all-reduce(bf16[768]{0:T(1024)(128)(2,1)S(1)} %dynamic-update-slice, ...), channel_id=5, replica_groups=mesh['fsdp'=8,'rep'=4] {'fsdp'}, use_global_device_ids=true, to_apply=%add.1 | all-reduce | flops 10752 | bytes 43008
  66.5 33.9 %all-gather.14 = bf16[1,384,384]{2,1,0:T(8,128)(2,1)} all-gather(bf16[1,48,384]{2,1,0:T(8,128)(2,1)S(1)} %get-tuple-element.118), channel_id=16, replica_groups=mesh['fsdp'=8,'rep'=4] {'fsdp'}, dimensions={1}, use_global_device_ids=true | all-gather | bytes 331776 | tf_op jit(solution)/shard_map/all_gather | solution.py:253
  100.4 31.4 %all-gather.4 = bf16[1,384,384]{2,1,0:T(8,128)(2,1)S(1)} all-gather(bf16[1,48,384]{2,1,0:T(8,128)(2,1)S(1)} %get-tuple-element.119), channel_id=6, replica_groups=mesh['fsdp'=8,'rep'=4] {'fsdp'}, dimensions={1}, use_global_device_ids=true | all-gather | bytes 331776 | tf_op jit(solution)/shard_map/all_gather | solution.py:253
  131.8 35.8 %all-gather.12 = bf16[1,384,1152]{2,1,0:T(8,128)(2,1)} all-gather(bf16[1,48,1152]{2,1,0:T(8,128)(2,1)S(1)} %get-tuple-element.110), channel_id=14, replica_groups=mesh['fsdp'=8,'rep'=4] {'fsdp'}, dimensions={1}, use_global_device_ids=true | all-gather | bytes 995328 | tf_op jit(solution)/shard_map/all_gather | solution.py:253
  167.6 35.7 %all-gather.2 = bf16[1,384,1152]{2,1,0:T(8,128)(2,1)} all-gather(bf16[1,48,1152]{2,1,0:T(8,128)(2,1)S(1)} %get-tuple-element.111), channel_id=4, replica_groups=mesh['fsdp'=8,'rep'=4] {'fsdp'}, dimensions={1}, use_global_device_ids=true | all-gather | bytes 995328 | tf_op jit(solution)/shard_map/all_gather | solution.py:253
  241.5 12.0 %multiply_convert_fusion.3 = (bf16[8,256,1536]{2,1,0:T(8,128)(2,1)}, f32[8,256,1536]{2,1,0:T(8,128)}) fusion(f32[1536]{0:T(1024)S(1)} %copy-done.78, bf16[1,384,1536]{2,1,0:T(8,128)(2,1)} %all-gather.29.cloned.1.call-done, f32[8,256,384]{2,1,0:T(8,128)} %copy-done.4, f32[8,384]{1,0:T(8,128)S(1)} %copy-done.60, f32[8,384]{1,0:T(8,128)S(1)} %get-tuple-element.122, ...), kind=kOutput, calls=%fused_computation.27 | convolution fusion | flops 2451308544 | bytes 23246848 | tf_op jit(solution)/shard_map/dot_general | solution.py:28
  295.7 11.1 multiply_convert_fusion.2
  306.8 14.5 %fusion.168 = (bf16[1536]{0:T(1024)(128)(2,1)}, bf16[8,256,1536]{2,1,0:T(8,128)(2,1)S(1)}) fusion(f32[8,256,1536]{2,1,0:T(8,128)} %get-tuple-element.146, f32[1536]{0:T(1024)} %convert_element_type.337, bf16[1,1536,384]{2,1,0:T(8,128)(2,1)} %all-gather.37.cloned.1.call-done, f32[8,256,384]{2,1,0:T(8,128)} %param.15, f32[8,384]{1,0:T(8,128)} %get-tuple-element.112), kind=kOutput, calls=%fused_computation.276 | convolution fusion | flops 2483550720 | bytes 23221248 | tf_op jit(solution)/shard_map/dot_general | solution.py:34
  345.3 9.6 bitcast_convert_fusion.2
  361.2 22.9 %fusion.85 = bf16[8,6,64,256]{3,2,1,0:T(8,128)(2,1)} fusion(bf16[8,256,6,64]{1,3,2,0:T(8,128)(2,1)} %bitcast.264, f32[8,6,256,256]{2,3,1,0:T(8,128)} %fusion.170, f32[8,6,256,256]{2,3,1,0:T(8,128)} %copy-done.1, f32[8,6,256]{2,1,0:T(8,128)S(1)} %log_add_fusion), kind=kOutput, calls=%fused_computation.139 | convolution fusion | flops 431763712 | bytes 28360704 | tf_op jit(solution)/shard_map/bhqk,bqhe->bkhe/dot_general | solution.py:23
  384.1 21.4 %bitcast_convert_fusion.3 = (bf16[8,256,6,64]{1,3,2,0:T(8,128)(2,1)}, f32[8,6,64,256]{3,2,1,0:T(8,128)}) fusion(bf16[8,256,6,64]{1,3,2,0:T(8,128)(2,1)} %bitcast.262, f32[8,6,256,256]{2,3,1,0:T(8,128)} %fusion.170, f32[8,6,256,256]{2,3,1,0:T(8,128)} %copy-done.1, f32[8,6,256]{2,1,0:T(8,128)S(1)} %log_add_fusion), kind=kOutput, calls=%fused_computation.61 | convolution fusion | flops 431763712 | bytes 31506432 | tf_op jit(solution)/shard_map/bhqk,bkhe->bqhe/dot_general | solution.py:23
  439.4 13.3 %fusion.169 = (bf16[1536]{0:T(1024)(128)(2,1)S(1)}, bf16[8,256,1536]{2,1,0:T(8,128)(2,1)S(1)}) fusion(f32[8,256,1536]{2,1,0:T(8,128)} %get-tuple-element.140, f32[1536]{0:T(1024)S(1)} %copy-done.79, bf16[1,1536,384]{2,1,0:T(8,128)(2,1)S(1)} %copy-done.97, f32[8,256,384]{2,1,0:T(8,128)S(1)} %get-tuple-element.85, f32[8,384]{1,0:T(8,128)S(1)} %get-tuple-element.120), kind=kOutput, calls=%fused_computation.277 | convolution fusion | flops 2483550720 | bytes 23221248 | tf_op jit(solution)/shard_map/dot_general | solution.py:34
  486.8 22.5 %bitcast_convert_fusion.1 = (bf16[8,256,6,64]{1,3,2,0:T(8,128)(2,1)S(1)}, f32[8,6,64,256]{3,2,1,0:T(8,128)}) fusion(bf16[8,256,6,64]{1,3,2,0:T(8,128)(2,1)S(1)} %bitcast.260, f32[8,6,256,256]{2,3,1,0:T(8,128)} %fusion.171, f32[8,6,256,256]{2,3,1,0:T(8,128)} %copy-done, f32[8,6,256]{2,1,0:T(8,128)S(1)} %copy-done.32), kind=kOutput, calls=%fused_computation.57 | convolution fusion | flops 431763712 | bytes 31506432 | tf_op jit(solution)/shard_map/bhqk,bkhe->bqhe/dot_general | solution.py:23
  510.9 22.3 %fusion.82 = bf16[8,6,64,256]{3,2,1,0:T(8,128)(2,1)} fusion(bf16[8,256,6,64]{1,3,2,0:T(8,128)(2,1)S(1)} %bitcast.258, f32[8,6,256,256]{2,3,1,0:T(8,128)} %fusion.171, f32[8,6,256,256]{2,3,1,0:T(8,128)} %copy-done, f32[8,6,256]{2,1,0:T(8,128)S(1)} %copy-done.32), kind=kOutput, calls=%fused_computation.138 | convolution fusion | flops 431763712 | bytes 28360704 | tf_op jit(solution)/shard_map/bhqk,bqhe->bkhe/dot_general | solution.py:23
  598.9 33.8 %all-reduce.20 = (bf16[2304]{0:T(1024)(128)(2,1)S(1)}, bf16[2304]{0:T(1024)(128)(2,1)S(1)}, bf16[768]{0:T(1024)(128)(2,1)S(1)}, bf16[768]{0:T(1024)(128)(2,1)S(1...) all-reduce(bf16[2304]{0:T(1024)(128)(2,1)S(1)} %reduce_sum.477, ...), channel_id=25, replica_groups=mesh['fsdp'=8,'rep'=4] {'fsdp'}, use_global_device_ids=true, to_apply=%region_42.43.clone | all-reduce | flops 10752 | bytes 43008
  650.3 31.7 %reduce-scatter.15.cloned.1.call-done = bf16[48,1152]{1,0:T(8,128)(2,1)} async-done(((bf16[384,1152]{1,0:T(8,128)(2,1)}), bf16[48,1152]{1,0:T(8,128)(2,1)}) %reduce-scatter.15.cloned.1.call-update) | async-done | bytes 110608 | tf_op jit(solution)/shard_map/reduce_scatter | solution.py:280
  682.0 67.0 %reduce-scatter.25.cloned.1.call-done = bf16[48,1536]{1,0:T(8,128)(2,1)} async-done(((bf16[384,1536]{1,0:T(8,128)(2,1)}), bf16[48,1536]{1,0:T(8,128)(2,1)}) %reduce-scatter.25.cloned.1.call-update) | async-done | bytes 147472 | tf_op jit(solution)/shard_map/reduce_scatter | solution.py:292
  749.0 66.9 %reduce-scatter.29.cloned.1.call-done = bf16[192,384]{1,0:T(8,128)(2,1)} async-done(((bf16[1536,384]{1,0:T(8,128)(2,1)}), bf16[192,384]{1,0:T(8,128)(2,1)}) %reduce-scatter.29.cloned.1.call-update) | async-done | bytes 147472 | tf_op jit(solution)/shard_map/reduce_scatter | solution.py:298
  816.0 67.1 %reduce-scatter.27.cloned.1.call-done = bf16[192,384]{1,0:T(8,128)(2,1)} async-done(((bf16[1536,384]{1,0:T(8,128)(2,1)}), bf16[192,384]{1,0:T(8,128)(2,1)}) %reduce-scatter.27.cloned.1.call-update) | async-done | bytes 147472 | tf_op jit(solution)/shard_map/reduce_scatter | solution.py:298
  883.1 66.9 %reduce-scatter.23.cloned.1.call-done = bf16[48,1536]{1,0:T(8,128)(2,1)} async-done(((bf16[384,1536]{1,0:T(8,128)(2,1)}), bf16[48,1536]{1,0:T(8,128)(2,1)}) %reduce-scatter.23.cloned.1.call-update) | async-done | bytes 147472 | tf_op jit(solution)/shard_map/reduce_scatter | solution.py:292
  950.0 69.0 %reduce-scatter.13.cloned.1.call-done = bf16[48,2304]{1,0:T(8,128)(2,1)} async-done(((bf16[384,2304]{1,0:T(8,128)(2,1)}), bf16[48,2304]{1,0:T(8,128)(2,1)}) %reduce-scatter.13.cloned.1.call-update) | async-done | bytes 221200 | tf_op jit(solution)/shard_map/reduce_scatter | solution.py:274
  1019.1 68.7 %reduce-scatter.11.cloned.1.call-done = bf16[48,2304]{1,0:T(8,128)(2,1)} async-done(((bf16[384,2304]{1,0:T(8,128)(2,1)}), bf16[48,2304]{1,0:T(8,128)(2,1)}) %reduce-scatter.11.cloned.1.call-update) | async-done | bytes 221200 | tf_op jit(solution)/shard_map/reduce_scatter | solution.py:274
  1087.8 34.5 %all-reduce.27.cloned.1.call-done = (bf16[1,288]{1,0:T(2,128)(2,1)}, bf16[1,288]{1,0:T(2,128)(2,1)}, bf16[1,96]{1,0:T(2,128)(2,1)}, bf16[1,96]{1,0:T(2,128)(2,1)...) async-done(((bf16[1,288]{1,0:T(2,128)(2,1)}, ...) | async-done | bytes 76432 | tf_op jit(solution)/shard_map/psum | solution.py:307
  1129.9 35.8 %all-reduce.29.cloned.1.call-done = (bf16[1,48,2304]{2,1,0:T(8,128)(2,1)}, bf16[1,48,2304]{2,1,0:T(8,128)(2,1)}, bf16[1,48,1152]{2,1,0:T(8,128)(2,1)}, bf16[1,48...) async-done(((bf16[1,48,2304]{2,1,0:T(8,128)(2,1)}, ...) | async-done | bytes 1253392 | tf_op jit(solution)/shard_map/psum | solution.py:306
  (429 shorter events, 291.4 us)
Async XLA Ops:
  7.3 196.7 %all-gather.27.cloned.1.call-start = ((), (), s32[]{:S(2)}) async-start(), calls=%async_computation.20 | async-start | bytes 1990656 | tf_op jit(solution)/shard_map/all_gather | solution.py:253
  9.3 197.1 %all-gather.33.cloned.1.call-start = ((), (), s32[]{:S(2)}) async-start(), calls=%async_computation.23 | async-start | bytes 1990656 | tf_op jit(solution)/shard_map/all_gather | solution.py:253
  10.1 231.4 %all-gather.29.cloned.1.call-start = ((), (), s32[]{:S(2)}) async-start(), calls=%async_computation.21 | async-start | bytes 1327104 | tf_op jit(solution)/shard_map/all_gather | solution.py:253
  11.9 241.7 %all-gather.31.cloned.1.call-start = ((), (), s32[]{:S(2)}) async-start(), calls=%async_computation.22 | async-start | bytes 1327104 | tf_op jit(solution)/shard_map/all_gather | solution.py:253
  13.7 282.1 %all-gather.35.cloned.1.call-start = ((), (), s32[]{:S(2)}) async-start(), calls=%async_computation.24 | async-start | bytes 1327104 | tf_op jit(solution)/shard_map/all_gather | solution.py:253
  14.3 292.5 %all-gather.37.cloned.1.call-start = ((), (), s32[]{:S(2)}) async-start(), calls=%async_computation.25 | async-start | bytes 1327104 | tf_op jit(solution)/shard_map/all_gather | solution.py:253
  14.8 631.8 %reduce-scatter.21.cloned.1.call-start = ((), (), s32[]{:S(2)}) async-start(), calls=%async_computation.15 | async-start | bytes 331776 | tf_op jit(solution)/shard_map/reduce_scatter | solution.py:286
  18.2 188.2 %copy-start.36 = (bf16[8,384]{1,0:T(8,128)(2,1)}, bf16[8,384]{1,0:T(8,128)(2,1)S(1)}, u32[]{:S(2)}) copy-start(bf16[8,384]{1,0:T(8,128)(2,1)S(1)} %multiply_convert_fusion.12) | copy-start | bytes 18436
  65.2 143.7 %copy-start.40 = (f32[8,256]{1,0:T(8,128)}, f32[8,256]{1,0:T(8,128)S(1)}, u32[]{:S(2)}) copy-start(f32[8,256]{1,0:T(8,128)S(1)} %broadcast_multiply_fusion.11) | copy-start | bytes 24580
  65.2 138.1 %copy-start.71 = (bf16[1,768]{1,0:T(2,128)(2,1)S(1)}, bf16[1,768]{1,0:T(2,128)(2,1)}, u32[]{:S(2)}) copy-start(bf16[1,768]{1,0:T(2,128)(2,1)} %reshape.387) | copy-start | bytes 4612
  65.2 138.1 %copy-start.72 = (bf16[1,768]{1,0:T(2,128)(2,1)S(1)}, bf16[1,768]{1,0:T(2,128)(2,1)}, u32[]{:S(2)}) copy-start(bf16[1,768]{1,0:T(2,128)(2,1)} %reshape.402) | copy-start | bytes 4612
  100.4 108.5 %copy-start.53 = (f32[8,256]{1,0:T(8,128)S(1)}, f32[8,256]{1,0:T(8,128)}, u32[]{:S(2)}) copy-start(f32[8,256]{1,0:T(8,128)} %add_rsqrt_fusion.3) | copy-start | bytes 24580
  131.8 104.0 %copy-start.27 = (bf16[1,384,384]{2,1,0:T(8,128)(2,1)}, bf16[1,384,384]{2,1,0:T(8,128)(2,1)S(1)}, u32[]{:S(2)}) copy-start(bf16[1,384,384]{2,1,0:T(8,128)(2,1)S(1)} %all-gather.4) | copy-start | bytes 884740
  433.3 213.3 %reduce-scatter.19.cloned.1.call-start = ((), (), s32[]{:S(2)}) async-start(), calls=%async_computation.14 | async-start | bytes 331776 | tf_op jit(solution)/shard_map/reduce_scatter | solution.py:286
  468.1 182.2 %reduce-scatter.17.cloned.1.call-start = ((), (), s32[]{:S(2)}) async-start(), calls=%async_computation.13 | async-start | bytes 995328 | tf_op jit(solution)/shard_map/reduce_scatter | solution.py:280
  477.7 204.3 %reduce-scatter.15.cloned.1.call-start = ((), (), s32[]{:S(2)}) async-start(), calls=%async_computation.12 | async-start | bytes 995328 | tf_op jit(solution)/shard_map/reduce_scatter | solution.py:280
  542.2 206.8 %reduce-scatter.25.cloned.1.call-start = ((), (), s32[]{:S(2)}) async-start(), calls=%async_computation.17 | async-start | bytes 1327104 | tf_op jit(solution)/shard_map/reduce_scatter | solution.py:292
  550.1 265.9 %reduce-scatter.29.cloned.1.call-start = ((), (), s32[]{:S(2)}) async-start(), calls=%async_computation.19 | async-start | bytes 1327104 | tf_op jit(solution)/shard_map/reduce_scatter | solution.py:298
  558.4 324.7 %reduce-scatter.27.cloned.1.call-start = ((), (), s32[]{:S(2)}) async-start(), calls=%async_computation.18 | async-start | bytes 1327104 | tf_op jit(solution)/shard_map/reduce_scatter | solution.py:298
  566.7 383.3 %reduce-scatter.23.cloned.1.call-start = ((), (), s32[]{:S(2)}) async-start(), calls=%async_computation.16 | async-start | bytes 1327104 | tf_op jit(solution)/shard_map/reduce_scatter | solution.py:292
  574.4 444.7 %reduce-scatter.13.cloned.1.call-start = ((), (), s32[]{:S(2)}) async-start(), calls=%async_computation.11 | async-start | bytes 1990656 | tf_op jit(solution)/shard_map/reduce_scatter | solution.py:274
  577.6 510.2 %reduce-scatter.11.cloned.1.call-start = ((), (), s32[]{:S(2)}) async-start(), calls=%async_computation.10 | async-start | bytes 1990656 | tf_op jit(solution)/shard_map/reduce_scatter | solution.py:274
  587.3 535.0 %all-reduce.27.cloned.1.call-start = ((), (), s32[]{:S(2)}) async-start(), calls=%async_computation.26 | async-start | bytes 163840 | tf_op jit(solution)/shard_map/psum | solution.py:307
  646.6 519.0 %all-reduce.29.cloned.1.call-start = ((), (), s32[]{:S(2)}) async-start(), calls=%async_computation.27 | async-start | bytes 2506752 | tf_op jit(solution)/shard_map/psum | solution.py:306
  (96 other events, 814.0 us)
Sparse Core Ops, SparseCore 0:
  10.8 49.4 all-gather.26
  63.0 47.2 all-gather.32
  113.1 45.0 all-gather.28
  160.2 43.9 all-gather.30
  206.8 39.9 all-gather.34
  248.8 39.7 all-gather.36
  433.4 56.8 reduce-scatter.20
  494.1 58.5 reduce-scatter.18
  556.6 61.1 reduce-scatter.16
  621.1 60.8 reduce-scatter.14
  685.4 63.5 reduce-scatter.24
  752.3 63.6 reduce-scatter.28
  819.4 63.6 reduce-scatter.26
  886.3 63.6 reduce-scatter.22
  953.3 65.6 reduce-scatter.12
  1022.4 65.3 reduce-scatter.10
  1092.0 30.2 all-reduce.26
  1125.1 40.5 all-reduce.28
where the time goes:
time: 1190 us; the launch traced here: 1180 us
  waiting for transfers between devices  510 us (43%)
  matrix products  311 us (26%)
  blocking collectives  210 us (18%)
  local copies, waits for them, and re-layouts  74.3 us (6%)
  other arithmetic  51.8 us (4%)
  between operations  21.3 us (2%)
    reduce_scatter x2, waiting for transfers between devices, body(): lax.psum_scatter(gradients[0].astype(jnp.bfloat16), 'fsdp', scatter_dimen...  138 us
    all_gather x4, blocking collectives, body(): lax.all_gather(as_sent(owned_rows), 'fsdp', axis=0, tiled=True)  137 us
    dot_general x12, matrix products, pair_product(): return jnp.einsum(form, left, right, preferred_element_type=jnp.float32)  136 us
    reduce_scatter x2, waiting for transfers between devices, body(): lax.psum_scatter(gradients[8].astype(jnp.bfloat16), 'fsdp', scatter_dimen...  134 us
    reduce_scatter x2, waiting for transfers between devices, body(): lax.psum_scatter(gradients[6].astype(jnp.bfloat16), 'fsdp', scatter_dimen...  134 us
    unnamed x2, blocking collectives  73.3 us
    dot_general x8, matrix products, matmul_back(): lax.dot_general(flattened, weight, (((1,), (1,)), ((), ())), preferred_el...  55.7 us
    dot_general x8, matrix products, matmul(): result = jnp.dot(flattened, weight, preferred_element_type=jnp.float32)  54.5 us
  transfers between devices with their start and end apart: 18, of which 9 were waited for; matrix products, arithmetic and copies ran while one was open for 25% of the time, Pallas kernels for 0%

commit v1 on v0

v1 whole, which is shorter than its diff:
```python
import functools

import jax
import jax.numpy as jnp
from jax import lax
from jax.experimental import pallas as pl
from jax.experimental.pallas import tpu as pltpu
from jax.sharding import PartitionSpec as P

GELU_C = 0.7978845608028654
GELU_A = 0.044715
EPS = 1e-06
HEAD = 64
LANES = 128
F32 = jnp.float32
BF16 = jnp.bfloat16


def dot(left, right, contract=((1,), (0,))):
    return lax.dot_general(left, right, (contract, ((), ())), preferred_element_type=F32)


def dot_t(left, right):
    return dot(left, right, ((1,), (1,)))


def row_mean(x):
    return jnp.sum(x, axis=-1, keepdims=True) * (1.0 / x.shape[-1])


def norm_rows(x):
    centered = x - row_mean(x)
    inverse = lax.rsqrt(row_mean(centered * centered) + EPS)
    return centered * inverse, inverse


def norm_back(grad, normed, inverse):
    return inverse * (grad - row_mean(grad) - normed * row_mean(grad * normed))


def col_sum(x):
    return jnp.sum(x, axis=0, keepdims=True)


def split_hi_lo(x):
    hi = x.astype(BF16)
    lo = (x - hi.astype(F32)).astype(BF16)
    return jnp.concatenate([hi, lo], axis=0)


def my_place():
    return lax.axis_index("fsdp"), lax.axis_index("rep") & 1


def weight_copies(pieces, rels, plan, sems):
    me, core = my_place()
    copies = []
    at = 0
    for piece, (rel_even, rel_odd, only) in zip(pieces, rels):
        rows = piece.shape[0]
        owner = me ^ jnp.where(core == 0, rel_even, rel_odd)
        for scratch, first, width, parts in plan:
            for part in range(parts):
                start = pl.multiple_of((owner * parts + part) * rows, rows)
                copies.append(
                    (
                        only,
                        pltpu.make_async_copy(
                            piece.at[:, pl.ds(first + part * width, width)],
                            scratch.at[pl.ds(start, rows), :],
                            sems.at[at],
                        ),
                    )
                )
                at += 1
    return copies


def on_place(only, action):
    if only is None:
        action()
    else:
        _, core = my_place()
        pl.when(core == only)(action)


class Columns:
    def __init__(self, rows, width, hidden):
        self.rows, self.width, self.hidden = rows, width, hidden
        self.parts = hidden // width
        w = width
        self.attn = {"ada": (0, 3 * w), "qkv": (3 * w, 3 * w), "out": (6 * w, w)}
        self.mlp = {"ada": (0, 3 * w), "up": (3 * w, hidden), "down": (3 * w + hidden, hidden)}
        self.attn_end = 7 * w
        self.mlp_end = 3 * w + 2 * hidden
        sizes = (6 * w, 3 * w, w, hidden, w)
        names = ("ada", "qkv", "out", "up", "down")
        self.bias, at = {}, 0
        for name, size in zip(names, sizes):
            self.bias[name] = (at, size)
            at += size
        self.bias_size = at
        self.attn_sums = {"ada": (0, 3 * w), "qv": (3 * w, 2 * w), "out": (5 * w, w)}
        self.mlp_sums = {"ada": (0, 3 * w), "up": (3 * w, hidden), "down": (3 * w + hidden, w)}
        self.attn_grad = self.even(self.attn_end + self.tiles(6 * w) * LANES)
        self.mlp_grad = self.even(self.mlp_end + self.tiles(4 * w + hidden) * LANES)

    def tiles(self, size):
        return -(-size // (LANES * self.rows))

    def even(self, columns):
        return -(-columns // (2 * LANES)) * 2 * LANES

    def attn_plan(self, base=0):
        w = self.width
        return [
            ((w, 3 * w), base + self.attn["ada"][0], 3 * w, 1),
            ((w, 3 * w), base + self.attn["qkv"][0], 3 * w, 1),
            ((w, w), base + self.attn["out"][0], w, 1),
        ]

    def mlp_plan(self, base=0):
        w, hidden = self.width, self.hidden
        return [
            ((w, 3 * w), base + self.mlp["ada"][0], 3 * w, 1),
            ((w, hidden), base + self.mlp["up"][0], hidden, 1),
            ((hidden, w), base + self.mlp["down"][0], w, self.parts),
        ]


def put_grad(refs, owner, first, value):
    me, _ = my_place()
    half_width = refs[0].shape[-1]
    width = value.shape[-1]
    for half in range(2):
        lo, hi = max(first, half * half_width), min(first + width, (half + 1) * half_width)
        if lo < hi:
            refs[half][owner ^ me, :, lo - half * half_width : hi - half * half_width] = value[
                :, lo - first : hi - first
            ].astype(BF16)


def put_sums(refs, tile_ref, rows, first):
    owners = refs[0].shape[0]
    for block in range(tile_ref.shape[0] // rows):
        tile = tile_ref[block * rows : (block + 1) * rows, :]
        for owner in range(owners):
            put_grad(refs, owner, first + block * LANES, tile)


def fill_sums(tile_ref, sums):
    tile_ref[...] = jnp.zeros_like(tile_ref)
    at = 0
    for row in sums:
        for lo in range(0, row.shape[-1], LANES):
            tile_ref[at : at + 1, :] = row[:, lo : lo + LANES]
            at += 1


def by_core(keep_ref, away_ref, write):
    _, core = my_place()

    @pl.when(core == 0)
    def _():
        write((keep_ref, away_ref))

    @pl.when(core != 0)
    def _():
        write((away_ref, keep_ref))


def lane_masks(tokens):
    lane = lax.broadcasted_iota(jnp.int32, (tokens, LANES), 1)
    return lane < HEAD, lane >= HEAD


def attn_fwd_body(args, weights, outs, per_step):
    s_ref, b_ada, b_qkv, b_out, h_ref = args
    w_ada, w_qkv, w_out = weights
    mod_ref, h2_ref, qkv_ref, p_ref, o_ref, y_ref = outs
    step = pl.program_id(0)
    width = h_ref.shape[-1]
    tokens = h_ref.shape[1]
    masks = lane_masks(tokens)
    zero = jnp.zeros((), BF16)

    @pl.when(step == 0)
    def _():
        mod_ref[...] = dot(s_ref[...], w_ada[...]) + b_ada

    for at in range(per_step):
        mod = mod_ref[pl.ds(step * per_step + at, 1), :]
        shift, scale, gate = (mod[:, i * width : (i + 1) * width] for i in range(3))
        h = h_ref[at]
        normed, _ = norm_rows(h)
        a = (normed * (1.0 + scale) + shift).astype(BF16)
        qkv = dot(a, w_qkv[...]) + b_qkv
        qkv_b = qkv.astype(BF16)
        qkv_ref[at] = qkv_b
        attended = []
        for pair in range(width // LANES):
            lo = pair * LANES
            query = (qkv[:, lo : lo + LANES] * 0.125).astype(BF16)
            key = qkv_b[:, width + lo : width + lo + LANES]
            value = qkv_b[:, 2 * width + lo : 2 * width + lo + LANES]
            total = None
            for e in range(2):
                scores = dot_t(query, jnp.where(masks[e], key, zero))
                top = jnp.max(scores, axis=-1, keepdims=True)
                grown = jnp.exp(scores - top)
                p = grown * (1.0 / jnp.sum(grown, axis=-1, keepdims=True))
                p_ref[at, 2 * pair + e] = p
                part = dot(p.astype(BF16), jnp.where(masks[e], value, zero))
                total = part if total is None else total + part
            attended.append(total.astype(BF16))
        o = jnp.concatenate(attended, axis=1)
        o_ref[at] = o
        y = dot(o, w_out[...]) + b_out
        y_ref[at] = y
        h2_ref[at] = h + gate * y


def mlp_fwd_body(args, weights, outs, per_step, chunk):
    s_ref, b_ada, b_up, b_down, h2_ref = args
    w_ada, w_up, w_down = weights
    mod_ref, h3_ref, m_ref, g_ref, slope_ref, z_ref = outs
    step = pl.program_id(0)
    width = h2_ref.shape[-1]
    hidden = w_up.shape[-1]

    @pl.when(step == 0)
    def _():
        mod_ref[...] = dot(s_ref[...], w_ada[...]) + b_ada

    for at in range(per_step):
        mod = mod_ref[pl.ds(step * per_step + at, 1), :]
        shift, scale, gate = (mod[:, i * width : (i + 1) * width] for i in range(3))
        h2 = h2_ref[at]
        normed, _ = norm_rows(h2)
        m = (normed * (1.0 + scale) + shift).astype(BF16)
        m_ref[at] = m
        z = None
        for first in range(0, hidden, chunk):
            span = slice(first, first + chunk)
            u = dot(m, w_up[:, span]) + b_up[:, span]
            square = u * u
            t = jnp.tanh(GELU_C * (u + GELU_A * (square * u)))
            half = 0.5 * (1.0 + t)
            g = (u * half).astype(BF16)
            slope_ref[at, :, span] = half + (0.5 * GELU_C) * u * (1.0 - t * t) * (
                1.0 + (3.0 * GELU_A) * square
            )
            g_ref[at, :, span] = g
            part = dot(g, w_down[span, :])
            z = part if z is None else z + part
        z = z + b_down
        z_ref[at] = z
        h3_ref[at] = h2 + gate * z


def mlp_bwd_body(args, weights, outs, accs, per_step, chunk, cols):
    s_ref, mod_ref, h2_ref, dh3_ref, m_ref, g_ref, slope_ref, z_ref = args
    w_ada, w_up, w_down = weights
    dcond_ref, keep_ref, away_ref, dh2_ref = outs
    acc_up, acc_down, dmod_ref, bias_ref, tile_ref, ada_ref, down_ref = accs
    step = pl.program_id(0)
    last = pl.num_programs(0) - 1
    width = h2_ref.shape[-1]
    hidden = w_up.shape[-1]

    @pl.when(step == 0)
    def _():
        acc_up[...] = jnp.zeros_like(acc_up)
        acc_down[...] = jnp.zeros_like(acc_down)
        bias_ref[...] = jnp.zeros_like(bias_ref)

    for at in range(per_step):
        row = step * per_step + at
        mod = mod_ref[pl.ds(row, 1), :]
        scale, gate = mod[:, width : 2 * width], mod[:, 2 * width : 3 * width]
        dh3 = dh3_ref[at]
        dz = gate * dh3
        dzb = dz.astype(BF16)
        dzb_t = dzb.T
        m_t = m_ref[at].T
        bias_ref[:, hidden : hidden + width] += col_sum(dz)
        dm = None
        for first in range(0, hidden, chunk):
            span = slice(first, first + chunk)
            du = dot_t(dzb, w_down[span, :]) * slope_ref[at, :, span]
            dub = du.astype(BF16)
            bias_ref[:, span] += col_sum(du)
            acc_down[:, span] += dot(dzb_t, g_ref[at, :, span])
            acc_up[:, span] += dot(m_t, dub)
            part = dot_t(dub, w_up[:, span])
            dm = part if dm is None else dm + part
        normed, inverse = norm_rows(h2_ref[at])
        dmod_ref[pl.ds(row, 1), :] = jnp.concatenate(
            [col_sum(dm), col_sum(dm * normed), col_sum(dh3 * z_ref[at])], axis=1
        )
        dh2_ref[at] = dh3 + norm_back(dm * (1.0 + scale), normed, inverse)

    @pl.when(step == last)
    def _():
        ada = ada_tail(s_ref, w_ada, dmod_ref, dcond_ref)
        ada_ref[...] = ada
        down_ref[...] = acc_down[...].T
        fill_sums(tile_ref, [col_sum(dmod_ref[...]), bias_ref[...]])
        rows = cols.rows

        def write(refs):
            for owner in range(refs[0].shape[0]):
                mine = slice(owner * rows, (owner + 1) * rows)
                put_grad(refs, owner, 0, ada_ref[mine, :])
                put_grad(refs, owner, cols.mlp["up"][0], acc_up[mine, :])
                for part in range(cols.parts):
                    first = (owner * cols.parts + part) * rows
                    put_grad(
                        refs,
                        owner,
                        cols.mlp["down"][0] + part * width,
                        down_ref[first : first + rows, :],
                    )
            put_sums(refs, tile_ref, rows, cols.mlp_end)

        by_core(keep_ref, away_ref, write)


def ada_tail(s_ref, w_ada, dmod_ref, dcond_ref):
    parts = split_hi_lo(dmod_ref[...])
    rows = dmod_ref.shape[0]
    both = dot_t(parts, w_ada[...])
    dcond_ref[...] = both[:rows] + both[rows:]
    s = s_ref[...]
    return dot(jnp.concatenate([s, s], axis=0), parts, ((0,), (0,)))


def attn_bwd_body(args, weights, outs, accs, per_step, cols):
    s_ref, mod_ref, h_ref, dh2_ref, qkv_ref, p_ref, o_ref, y_ref = args
    w_ada, w_qkv, w_out = weights
    dcond_ref, keep_ref, away_ref, dh_ref = outs
    acc_qkv, acc_out, dqkv_ref, dmod_ref, bias_ref, tile_ref, ada_ref = accs
    step = pl.program_id(0)
    last = pl.num_programs(0) - 1
    width = h_ref.shape[-1]
    tokens = h_ref.shape[1]
    masks = lane_masks(tokens)
    zero = jnp.zeros((), BF16)

    @pl.when(step == 0)
    def _():
        acc_qkv[...] = jnp.zeros_like(acc_qkv)
        acc_out[...] = jnp.zeros_like(acc_out)
        bias_ref[...] = jnp.zeros_like(bias_ref)

    for at in range(per_step):
        row = step * per_step + at
        mod = mod_ref[pl.ds(row, 1), :]
        shift, scale, gate = (mod[:, i * width : (i + 1) * width] for i in range(3))
        dh2 = dh2_ref[at]
        dy = gate * dh2
        dyb = dy.astype(BF16)
        bias_ref[:, 2 * width : 3 * width] += col_sum(dy)
        acc_out[...] += dot(o_ref[at].T, dyb)
        do = dot_t(dyb, w_out[...]).astype(BF16)
        do_t = do.T
        query_t = qkv_ref[at, :, :width].T
        dk_t, dv_t = [], []
        for pair in range(width // LANES):
            lo = pair * LANES
            key = qkv_ref[at, :, width + lo : width + lo + LANES]
            value = qkv_ref[at, :, 2 * width + lo : 2 * width + lo + LANES]
            do_pair = do[:, lo : lo + LANES]
            dq = None
            for e in range(2):
                head = 2 * pair + e
                rows = slice(head * HEAD, (head + 1) * HEAD)
                p = p_ref[at, head]
                dp = dot_t(do_pair, jnp.where(masks[e], value, zero))
                inner = jnp.sum(p * dp, axis=-1, keepdims=True)
                ds = (p * (dp - inner) * 0.125).astype(BF16)
                dv_t.append(dot(do_t[rows], p.astype(BF16)))
                dk_t.append(dot(query_t[rows], ds))
                part = dot(ds, jnp.where(masks[e], key, zero))
                dq = part if dq is None else dq + part
            bias_ref[:, lo : lo + LANES] += col_sum(dq)
            dqkv_ref[:, lo : lo + LANES] = dq.astype(BF16)
        dv = jnp.concatenate(dv_t, axis=0).T
        bias_ref[:, width : 2 * width] += col_sum(dv)
        dqkv_ref[:, width : 2 * width] = jnp.concatenate(dk_t, axis=0).T.astype(BF16)
        dqkv_ref[:, 2 * width :] = dv.astype(BF16)
        normed, inverse = norm_rows(h_ref[at])
        a = (normed * (1.0 + scale) + shift).astype(BF16)
        acc_qkv[...] += dot(a.T, dqkv_ref[...])
        da = dot_t(dqkv_ref[...], w_qkv[...])
        dmod_ref[pl.ds(row, 1), :] = jnp.concatenate(
            [col_sum(da), col_sum(da * normed), col_sum(dh2 * y_ref[at])], axis=1
        )
        dh_ref[at] = dh2 + norm_back(da * (1.0 + scale), normed, inverse)

    @pl.when(step == last)
    def _():
        ada = ada_tail(s_ref, w_ada, dmod_ref, dcond_ref)
        ada_ref[...] = ada
        fill_sums(tile_ref, [col_sum(dmod_ref[...]), bias_ref[...]])
        rows = cols.rows

        def write(refs):
            for owner in range(refs[0].shape[0]):
                mine = slice(owner * rows, (owner + 1) * rows)
                put_grad(refs, owner, 0, ada_ref[mine, :])
                put_grad(refs, owner, cols.attn["qkv"][0], acc_qkv[mine, :])
                put_grad(refs, owner, cols.attn["out"][0], acc_out[mine, :])
            put_sums(refs, tile_ref, rows, cols.attn_end)

        by_core(keep_ref, away_ref, write)


def per_latent(shape, per_step):
    rest = shape[1:]
    return pl.BlockSpec((per_step,) + rest, lambda b: (b,) + (0,) * len(rest))


def whole(shape):
    return pl.BlockSpec(shape, lambda b: (0,) * len(shape))


def sds(shape, dtype=F32):
    return jax.ShapeDtypeStruct(tuple(shape), dtype)


def params(steps=True):
    return pltpu.CompilerParams(
        dimension_semantics=("arbitrary",) if steps else None, vmem_limit_bytes=60 * 2**20
    )


def estimate(micros):
    return pl.CostEstimate(flops=int(micros * 1.0e9), bytes_accessed=int(micros * 1.0e6), transcendentals=0)


def run(body, constants, streams, gathered, plan, out_constants, out_streams, scratch, per_step, name, micros):
    latents = streams[0].shape[0]
    pieces, rels = gathered
    direct = rels is None
    n_in = len(constants) + len(streams)
    n_out = len(out_streams) + len(out_constants)
    copies = 0 if direct else len(pieces) * sum(parts for _, _, _, parts in plan)

    def kernel(*refs):
        ins, rest = refs[:n_in], refs[n_in:]
        got, rest = rest[: len(pieces)], rest[len(pieces) :]
        outs, rest = rest[:n_out], rest[n_out:]
        if direct:
            weights, accs = got, rest
        else:
            weights, sems, accs = rest[: len(plan)], rest[len(plan)], rest[len(plan) + 1 :]

            @pl.when(pl.program_id(0) == 0)
            def _():
                started = weight_copies(
                    got, rels, [(w,) + tuple(p[1:]) for w, p in zip(weights, plan)], sems
                )
                for only, copy in started:
                    on_place(only, copy.start)
                for only, copy in started:
                    on_place(only, copy.wait)

        body(ins, weights, outs, accs)

    if direct:
        piece_specs = [whole(p.shape) for p in pieces]
        extra = []
    else:
        piece_specs = [pl.BlockSpec(memory_space=pl.ANY)] * len(pieces)
        extra = [pltpu.VMEM(shape, BF16) for shape, _, _, _ in plan]
        extra.append(pltpu.SemaphoreType.DMA((copies,)))
    return pl.pallas_call(
        kernel,
        grid=(latents // per_step,),
        in_specs=[whole(c.shape) for c in constants]
        + [per_latent(x.shape, per_step) for x in streams]
        + piece_specs,
        out_specs=[whole(x.shape) for x in out_constants]
        + [per_latent(x.shape, per_step) for x in out_streams],
        out_shape=list(out_constants) + list(out_streams),
        scratch_shapes=extra + list(scratch),
        compiler_params=params(),
        cost_estimate=estimate(micros),
        name=name,
    )(*constants, *streams, *pieces)


def layer_bias(bias_ref, cols, layer, name, part=None):
    first, size = cols.bias[name]
    first += layer * cols.bias_size
    if part is not None:
        size //= 2
        first += part * size
    return bias_ref[:, first : first + size]


def attn_fwd(h, s, bias, gathered, plan, cols, layer, per_step=1):
    n, tokens, width = h.shape

    def body(ins, weights, outs, _):
        s_ref, bias_ref, h_ref = ins
        biases = (
            layer_bias(bias_ref, cols, layer, "ada", 0),
            layer_bias(bias_ref, cols, layer, "qkv"),
            layer_bias(bias_ref, cols, layer, "out"),
        )
        attn_fwd_body((s_ref,) + biases + (h_ref,), weights, outs, per_step)

    return run(
        body,
        [s, bias],
        [h],
        gathered,
        plan,
        [sds((n, 3 * width))],
        [
            sds(h.shape),
            sds((n, tokens, 3 * width), BF16),
            sds((n, width // HEAD, tokens, tokens)),
            sds(h.shape, BF16),
            sds(h.shape),
        ],
        [],
        per_step,
        "attn_fwd",
        20,
    )


def mlp_fwd(h2, s, bias, gathered, plan, cols, layer, per_step=1, chunk=256):
    n, tokens, width = h2.shape
    hidden = cols.hidden

    def body(ins, weights, outs, _):
        s_ref, bias_ref, h2_ref = ins
        biases = (
            layer_bias(bias_ref, cols, layer, "ada", 1),
            layer_bias(bias_ref, cols, layer, "up"),
            layer_bias(bias_ref, cols, layer, "down"),
        )
        mlp_fwd_body((s_ref,) + biases + (h2_ref,), weights, outs, per_step, chunk)

    return run(
        body,
        [s, bias],
        [h2],
        gathered,
        plan,
        [sds((n, 3 * width))],
        [
            sds(h2.shape),
            sds(h2.shape, BF16),
            sds((n, tokens, hidden), BF16),
            sds((n, tokens, hidden)),
            sds(h2.shape),
        ],
        [],
        per_step,
        "mlp_fwd",
        22,
    )


def mlp_bwd(s, mod, h2, dh3, m, g, slope, z, gathered, plan, cols, owners, per_step=1, chunk=256):
    n, tokens, width = h2.shape
    hidden = cols.hidden

    def body(ins, weights, outs, accs):
        mlp_bwd_body(ins, weights, outs, accs, per_step, chunk, cols)

    return run(
        body,
        [s, mod],
        [h2, dh3, m, g, slope, z],
        gathered,
        plan,
        [sds((n, width))] + [sds((owners, cols.rows, cols.mlp_grad // 2), BF16)] * 2,
        [sds(h2.shape)],
        [
            pltpu.VMEM((width, hidden), F32),
            pltpu.VMEM((width, hidden), F32),
            pltpu.VMEM((n, 3 * width), F32),
            pltpu.VMEM((1, hidden + width), F32),
            pltpu.VMEM((cols.tiles(4 * width + hidden) * cols.rows, LANES), F32),
            pltpu.VMEM((width, 3 * width), F32),
            pltpu.VMEM((hidden, width), F32),
        ],
        per_step,
        "mlp_bwd",
        24,
    )


def attn_bwd(s, mod, h, dh2, qkv, p, o, y, gathered, plan, cols, owners, per_step=1):
    n, tokens, width = h.shape

    def body(ins, weights, outs, accs):
        attn_bwd_body(ins, weights, outs, accs, per_step, cols)

    return run(
        body,
        [s, mod],
        [h, dh2, qkv, p, o, y],
        gathered,
        plan,
        [sds((n, width))] + [sds((owners, cols.rows, cols.attn_grad // 2), BF16)] * 2,
        [sds(h.shape)],
        [
            pltpu.VMEM((width, 3 * width), F32),
            pltpu.VMEM((width, width), F32),
            pltpu.VMEM((tokens, 3 * width), BF16),
            pltpu.VMEM((n, 3 * width), F32),
            pltpu.VMEM((1, 3 * width), F32),
            pltpu.VMEM((cols.tiles(6 * width) * cols.rows, LANES), F32),
            pltpu.VMEM((width, 3 * width), F32),
        ],
        per_step,
        "attn_bwd",
        28,
    )


def simple_call(kernel, args, outs, name, scratch=()):
    vmem = pl.BlockSpec(memory_space=pltpu.VMEM)
    return pl.pallas_call(
        kernel,
        in_specs=[vmem] * len(args),
        out_specs=[vmem] * len(outs),
        out_shape=list(outs),
        scratch_shapes=list(scratch),
        compiler_params=params(False),
        cost_estimate=estimate(1),
        name=name,
    )(*args)


def pack_shards(stacked, cols, owners, layers):
    rows, width, hidden = cols.rows, cols.width, cols.hidden
    tiles = cols.tiles(layers * cols.bias_size)
    names = ("ada", "qkv", "out", "up", "down")

    def kernel(w_ada, b_ada, w_qkv, qv_bias, w_out, b_out, w_up, b_up, w_down, b_down, *refs):
        outs, row_ref, tile_ref = refs[:-2], refs[-2], refs[-1]
        me, _ = my_place()
        for layer in range(layers):
            attn_ref = outs[0] if layer == 0 else outs[layer + 1]
            mlp_ref = outs[1] if layer == 0 else outs[layer + 1]
            base = 0 if layer == 0 else cols.attn_end
            attn_ref[:, : 3 * width] = w_ada[layer, :, : 3 * width]
            attn_ref[:, 3 * width : 6 * width] = w_qkv[layer]
            attn_ref[:, 6 * width : 7 * width] = w_out[layer]
            mlp_ref[:, base : base + 3 * width] = w_ada[layer, :, 3 * width :]
            first = base + 3 * width
            mlp_ref[:, first : first + hidden] = w_up[layer]
            first += hidden
            for part in range(cols.parts):
                mlp_ref[:, first + part * width : first + (part + 1) * width] = w_down[
                    layer, part * rows : (part + 1) * rows, :
                ]
        row_ref[...] = jnp.zeros_like(row_ref)
        for owner in range(owners):

            @pl.when(me == owner)
            def _():
                for layer in range(layers):
                    for name, ref in zip(names, (b_ada, qv_bias, b_out, b_up, b_down)):
                        size = ref.shape[-1]
                        at = layer * cols.bias_size + cols.bias[name][0] + owner * size
                        if name == "qkv" and 2 * owner >= owners:
                            at += width
                        row_ref[:, at : at + size] = ref[layer : layer + 1, :].astype(F32)

        tile_ref[...] = jnp.zeros_like(tile_ref)
        for at in range(layers * cols.bias_size // LANES):
            tile_ref[at : at + 1, :] = row_ref[:, at * LANES : (at + 1) * LANES]
        for tile in range(tiles):
            outs[0][:, cols.attn_end + tile * LANES : cols.attn_end + (tile + 1) * LANES] = tile_ref[
                tile * rows : (tile + 1) * rows, :
            ].astype(BF16)

    outs = [sds((rows, cols.attn_end + tiles * LANES), BF16), sds((rows, cols.mlp_end), BF16)]
    outs += [sds((rows, cols.attn_end + cols.mlp_end), BF16)] * (layers - 1)
    scratch = [pltpu.VMEM((1, layers * cols.bias_size), F32), pltpu.VMEM((tiles * rows, LANES), F32)]
    return simple_call(kernel, stacked, outs, "pack", scratch)


def sum_bias(tiles, cols, layers, only_of):
    rows = cols.rows

    def kernel(*refs):
        ins, out_ref, sum_ref = refs[:-2], refs[-2], refs[-1]
        _, core = my_place()
        total = None
        for ref, only in zip(ins, only_of):
            value = ref[...].astype(F32)
            if only is not None:
                value = jnp.where(core == only, value, 0.0)
            total = value if total is None else total + value
        for tile in range(total.shape[1] // LANES):
            sum_ref[tile * rows : (tile + 1) * rows, :] = total[:, tile * LANES : (tile + 1) * LANES]
        for at in range(layers * cols.bias_size // LANES):
            out_ref[:, at * LANES : (at + 1) * LANES] = sum_ref[at : at + 1, :]

    count = tiles[0].shape[1] // LANES
    (out,) = simple_call(
        kernel,
        tiles,
        [sds((1, layers * cols.bias_size))],
        "sum_bias",
        [pltpu.VMEM((count * rows, LANES), F32)],
    )
    return out


class Slice:
    def __init__(self, mesh):
        self.owners, self.reps = mesh.shape["fsdp"], mesh.shape["rep"]

    def send(self, x, rel_even=0, rel_odd=None, swap=0, only=None):
        rel_odd = rel_even if rel_odd is None else rel_odd
        pairs = []
        for f in range(self.owners):
            for r in range(self.reps):
                rel = rel_odd if r & 1 else rel_even
                if only is None or (r & 1) == only:
                    pairs.append((f * self.reps + r, (f ^ rel) * self.reps + (r ^ swap)))
        return lax.ppermute(x, ("fsdp", "rep"), pairs)


def can_share(slc, rows):
    return slc.owners == 8 and slc.reps % 2 == 0 and rows % 16 == 0


RELS = (
    (0, 0, None),
    (2, 4, None),
    (6, 1, None),
    (4, 2, None),
    (1, 6, None),
    (3, 5, None),
    (5, 3, None),
    (7, 7, 0),
    (7, 7, 1),
)


def gather(piece, slc):
    first, second = yield (slc.send(piece, 2, 4), slc.send(piece, 6, 1))
    first_x, second_x = slc.send(first, swap=1), slc.send(second, swap=1)
    third, fourth = slc.send(first, 1, 1), slc.send(second, 1, only=0)
    first_x, second_x, third, fourth = yield (first_x, second_x, third, fourth)
    third_x, fourth_x = yield (slc.send(third, swap=1), slc.send(fourth, swap=1, only=0))
    return (piece, first, second, first_x, second_x, third, third_x, fourth, fourth_x), RELS


def whole_weights(full, plan):
    weights = []
    for (depth, width), first, part_width, parts in plan:
        block = full[:, :, first : first + part_width * parts]
        if parts > 1:
            owners, rows, _ = block.shape
            block = block.reshape(owners, rows, parts, part_width).transpose(0, 2, 1, 3)
        weights.append(block.reshape(depth, width))
    return weights, None


def add_split(left, right, picks):
    rest = left.shape[1:]

    def kernel(l_ref, r_ref, *outs):
        for out, pick in zip(outs, picks):
            for at, (a, b) in enumerate(pick):
                out[at] = (l_ref[a].astype(F32) + r_ref[b].astype(F32)).astype(out.dtype)

    return simple_call(kernel, [left, right], [sds((len(p),) + rest, BF16) for p in picks], "add_split")


def add_all(parts, dtype):
    def kernel(*refs):
        total = refs[0][...].astype(F32)
        for ref in refs[1:-1]:
            total += ref[...].astype(F32)
        refs[-1][...] = total.astype(dtype)

    (out,) = simple_call(kernel, parts, [sds(parts[0].shape, dtype)], "add_all")
    return out


def scatter_sum(keep, away, slc):
    owners = slc.owners
    (got,) = yield (slc.send(away, swap=1),)
    odd, even = add_split(
        keep,
        got,
        [[(j, j) for j in range(1, owners, 2)], [(j, j) for j in range(0, owners, 2)]],
    )
    got, even = yield (slc.send(odd, 1), even)
    blocks = add_split(even, got, [[(j, j)] for j in range(owners // 2)])
    arrived = yield (blocks[0],) + tuple(slc.send(blocks[j], 2 * j) for j in range(1, owners // 2))
    total = add_all(arrived, BF16)
    swap = 2
    while swap < slc.reps:
        total, got = yield (total, slc.send(total, swap=swap))
        total = add_all([total, got], BF16)
        swap *= 2
    total, other = yield (total, slc.send(total, swap=1))
    return total[0], other[0]


class Chain:
    def __init__(self, steps):
        self.steps, self.result = steps, None
        self.pending = next(steps)

    def step(self, arrived):
        try:
            self.pending = self.steps.send(arrived)
        except StopIteration as end:
            self.pending, self.result = None, end.value

    def finish(self):
        while self.pending is not None:
            self.step(self.pending)
        return self.result


def advance(chains, tied):
    live = [chain for chain in chains if chain.pending is not None]
    tied, arrived = lax.optimization_barrier((tied, [chain.pending for chain in live]))
    for chain, got in zip(live, arrived):
        chain.step(tuple(got))
    return tied


def unpack(halves, cols, owners, layers):
    rows, width, hidden = cols.rows, cols.width, cols.hidden

    def kernel(*refs):
        ins = refs[: 4 * layers]
        w_ada, b_ada, w_qkv, qv_bias, w_out, b_out, w_up, b_up, w_down, b_down, row_ref = refs[4 * layers :]
        me, core = my_place()

        def take(pair, first, size):
            half_width = pair[0].shape[-1]
            parts = []
            for half in range(2):
                lo, hi = max(first, half * half_width), min(first + size, (half + 1) * half_width)
                if lo < hi:
                    parts.append(pair[half][:, lo - half * half_width : hi - half * half_width])
            return jnp.concatenate(parts, axis=1).astype(F32) if len(parts) > 1 else parts[0].astype(F32)

        def write(layer, attn, mlp):
            w_ada[layer, :, : 3 * width] = take(attn, 0, 3 * width)
            w_qkv[layer] = take(attn, *cols.attn["qkv"])
            w_out[layer] = take(attn, *cols.attn["out"])
            w_ada[layer, :, 3 * width :] = take(mlp, 0, 3 * width)
            w_up[layer] = take(mlp, *cols.mlp["up"])
            for part in range(cols.parts):
                w_down[layer, part * rows : (part + 1) * rows, :] = take(
                    mlp, cols.mlp["down"][0] + part * width, width
                )
            at = 0
            for pair, first, size in (
                (attn, cols.attn_end, 6 * width),
                (mlp, cols.mlp_end, 4 * width + hidden),
            ):
                tiles = [
                    take(pair, first + t * LANES, LANES) for t in range(cols.tiles(size))
                ]
                for line in range(size // LANES):
                    row_ref[layer : layer + 1, at : at + LANES] = tiles[line // rows][
                        line % rows : line % rows + 1, :
                    ]
                    at += LANES

        for layer in range(layers):
            attn, mlp = ins[4 * layer : 4 * layer + 2], ins[4 * layer + 2 : 4 * layer + 4]

            @pl.when(core == 0)
            def _():
                write(layer, attn, mlp)

            @pl.when(core == 1)
            def _():
                write(layer, attn[::-1], mlp[::-1])

        w = width
        ada = jnp.concatenate([row_ref[:, : 3 * w], row_ref[:, 6 * w : 9 * w]], axis=1)
        qv = row_ref[:, 3 * w : 5 * w]
        out = row_ref[:, 5 * w : 6 * w]
        up = row_ref[:, 9 * w : 9 * w + hidden]
        down = row_ref[:, 9 * w + hidden : 10 * w + hidden]
        for owner in range(owners):

            @pl.when(me == owner)
            def _():
                for ref, value in ((b_ada, ada), (qv_bias, qv), (b_out, out), (b_up, up), (b_down, down)):
                    size = ref.shape[-1]
                    ref[...] = value[:, owner * size : (owner + 1) * size]

    outs = [
        sds((layers, rows, 6 * width)),
        sds((layers, 6 * width // owners)),
        sds((layers, rows, 3 * width)),
        sds((layers, 2 * width // owners)),
        sds((layers, rows, width)),
        sds((layers, width // owners)),
        sds((layers, rows, hidden)),
        sds((layers, hidden // owners)),
        sds((layers, rows * cols.parts, width)),
        sds((layers, width // owners)),
    ]
    args = [x for group in halves for x in group]
    return simple_call(
        kernel, args, outs, "unpack", [pltpu.VMEM((layers, 10 * width + hidden), F32)]
    )


def program(slc, latents, condition, cotangent, *stacked):
    layers = stacked[0].shape[0]
    width = latents.shape[-1]
    rows = stacked[2].shape[1]
    hidden = stacked[6].shape[-1]
    owners = slc.owners
    cols = Columns(rows, width, hidden)
    packed = pack_shards(stacked, cols, owners, layers)
    tiles = cols.tiles(layers * cols.bias_size) * LANES

    plans = []
    for layer in range(layers):
        base = 0 if layer == 0 else cols.attn_end
        plans.append((cols.attn_plan(), cols.mlp_plan(base)))
    s = jax.nn.silu(condition).astype(BF16)
    shared = can_share(slc, rows)
    if shared:
        now, chains = Chain(gather(packed[0], slc)), []
        waiting = list(packed[1:])
        waiting[0] = advance([now], waiting[0])
        chains.append(Chain(gather(waiting.pop(0), slc)))
        first = now.finish()
        bias_tiles = [piece[:, cols.attn_end :] for piece in first[0]]
        only_of = [only for _, _, only in first[1]]
    else:
        full = [lax.all_gather(piece, "fsdp", axis=0, tiled=False) for piece in packed]
        places = [(full[0], full[1])] + [(x, x) for x in full[2:]]
        whole_groups = [
            (whole_weights(a, pa), whole_weights(m, pm)) for (a, m), (pa, pm) in zip(places, plans)
        ]
        bias_tiles = [full[0][owner, :, cols.attn_end :] for owner in range(owners)]
        only_of = [None] * owners
    bias = sum_bias(bias_tiles, cols, layers, only_of)

    h = latents
    saved = []
    for layer in range(layers):
        attn_plan, mlp_plan = plans[layer]
        attn = (first if layer == 0 else chains[layer].finish()) if shared else whole_groups[layer][0]
        mod1, h2, qkv, p, o, y = attn_fwd(h, s, bias, attn, attn_plan, cols, layer)
        if shared and layer == 0:
            h2, waiting = advance(chains, (h2, waiting))
            chains += [Chain(gather(piece, slc)) for piece in waiting]
        if shared:
            mlp = chains[layer if layer else 0].finish()
        else:
            mlp = whole_groups[layer][1]
        mod2, h3, m, g, slope, z = mlp_fwd(h2, s, bias, mlp, mlp_plan, cols, layer)
        if shared:
            h3 = advance(chains, h3)
        saved.append((h, attn, mlp, mod1, h2, qkv, p, o, y, mod2, m, g, slope, z))
        h = h3
    output = h

    grad = cotangent
    grad_silu = None
    chains = []
    for layer in reversed(range(layers)):
        attn_plan, mlp_plan = plans[layer]
        h, attn, mlp, mod1, h2, qkv, p, o, y, mod2, m, g, slope, z = saved[layer]
        cond2, keep, away, grad = mlp_bwd(
            s, mod2, h2, grad, m, g, slope, z, mlp, mlp_plan, cols, owners
        )
        grad, keep, away = advance(chains, (grad, keep, away))
        chains.append(Chain(scatter_sum(keep, away, slc)))
        grad = advance(chains[-1:], grad)
        cond1, keep, away, grad = attn_bwd(
            s, mod1, h, grad, qkv, p, o, y, attn, attn_plan, cols, owners
        )
        grad, keep, away = advance(chains, (grad, keep, away))
        chains.append(Chain(scatter_sum(keep, away, slc)))
        grad = advance(chains[-1:], grad)
        both = cond1 + cond2
        grad_silu = both if grad_silu is None else grad_silu + both
    done = [chain.finish() for chain in chains]
    halves = [done[2 * (layers - 1 - layer) + 1] + done[2 * (layers - 1 - layer)] for layer in range(layers)]
    sigmoid_c = jax.nn.sigmoid(condition)
    grad_cond = grad_silu * sigmoid_c * (1.0 + condition * (1.0 - sigmoid_c))
    return (output, grad, grad_cond) + tuple(unpack(halves, cols, owners, layers))


def solution(mesh):
    rows3 = P(("fsdp", "rep"), None, None)
    rows2 = P(("fsdp", "rep"), None)
    pair = (P(None, "fsdp", None), P(None, "fsdp"))
    return jax.shard_map(
        functools.partial(program, Slice(mesh)),
        mesh=mesh,
        in_specs=(rows3, rows2, rows3) + pair * 5,
        out_specs=(rows3, rows3, rows2) + pair * 5,
        check_vma=False,
    )
```

time: 1190 us -> 390 us (0.33)
  waiting for transfers between devices: 510 us -> 60 us
  matrix products: 311 us -> 0 us
  Pallas kernels: 0 us -> 244 us
  blocking collectives: 210 us -> 0 us
  starting transfers between devices: 1.52 us -> 60.6 us
  local copies, waits for them, and re-layouts: 74.3 us -> 20.6 us
  other arithmetic: 51.8 us -> 1.22 us
  between operations: 21.3 us -> 1.33 us
    reduce_scatter x10 -> x0, waiting for transfers between devices: 438 us -> none  [the longest x2 138 us: body(): lax.psum_scatter(gradients[0].astype(jnp.bfloat16), 'fsdp', scatter_dimen...]
    dot_general x42 -> x0, matrix products: 311 us -> none  [the longest x12 136 us: pair_product(): return jnp.einsum(form, left, right, preferred_element_type=jnp.float32)]
    pallas_call x0 -> x27, Pallas kernels: none -> 244 us  [the longest x8 201 us: run(): pl.pallas_call(kernel, grid=(latents // per_step,), in_specs=[whole(c.sha...]
    all_gather x4 -> x0, blocking collectives: 137 us -> none  [body(): lax.all_gather(as_sent(owned_rows), 'fsdp', axis=0, tiled=True)]
    unnamed x2 -> x0, blocking collectives: 73.3 us -> none
    psum x2 -> x0, waiting for transfers between devices: 70.3 us -> none  [the longest x1 35.8 us: body(): lax.psum(owned_sums[0].astype(jnp.bfloat16), 'rep').astype(jnp.float32)]
    ppermute x0 -> x52, starting transfers between devices: none -> 60.6 us  [send(): return lax.ppermute(x, ('fsdp', 'rep'), pairs)]
    ppermute x0 -> x52, waiting for transfers between devices: none -> 60 us  [send(): return lax.ppermute(x, ('fsdp', 'rep'), pairs)]
  transfers between devices with their start and end apart: 18 -> 52, of which waited for: 9 -> 14; matrix products, arithmetic and copies ran while one was open for 25% -> 2% of each run, Pallas kernels for 0% -> 41%
where the time goes in v1:
time: 390 us; the launch traced here: 388 us
  Pallas kernels  244 us (63%)
  starting transfers between devices  60.6 us (16%)
  waiting for transfers between devices  60 us (15%)
  local copies, waits for them, and re-layouts  20.6 us (5%)
    pallas_call x8, Pallas kernels, run(): pl.pallas_call(kernel, grid=(latents // per_step,), in_specs=[whole(c.sha...  201 us
    ppermute x52, starting transfers between devices, send(): return lax.ppermute(x, ('fsdp', 'rep'), pairs)  60.6 us
    ppermute x52, waiting for transfers between devices, send(): return lax.ppermute(x, ('fsdp', 'rep'), pairs)  60 us
    pallas_call x19, Pallas kernels, simple_call(): pl.pallas_call(kernel, in_specs=[vmem] * len(args), out_specs=[vmem] * le...  42.6 us
    unnamed x112, local copies, waits for them, and re-layouts  14.3 us
  transfers between devices with their start and end apart: 52, of which 14 were waited for; matrix products, arithmetic and copies ran while one was open for 2% of the time, Pallas kernels for 41%

profile of v1, /device:TPU:0, one launch (start us, length us, event | category | flops | bytes accessed | tf_op | source)
XLA Modules:
  0.0 387.7 jit_solution(3184433385130172967)
XLA Ops:
  3.2 5.1 %collective-permute-start.1 = (bf16[48,2944]{1,0:T(8,128)(2,1)}, bf16[48,2944]{1,0:T(8,128)(2,1)S(1)}, u32[]{:S(2)}, u32[]{:S(2)}) collective-permute-start(bf16[48,2944]{1,0:T(8,128)(2,1)} %get-tuple-element.136.refs_3_.refs_8_), channel_id=1, source_target_pairs={{0,24},{1,5},{2,26},{3,7},{4,28},{5,1},{6,30},{7,3},{8,16},{9,13},... | collective-permute-start | bytes 847880 | tf_op jit(solution)/shard_map/ppermute | solution.py:733
  8.4 7.5 %collective-permute-done.1.refs_5_.refs_10_ = bf16[48,2944]{1,0:T(8,128)(2,1)S(1)} collective-permute-done((bf16[48,2944]{1,0:T(8,128)(2,1)}, bf16[48,2944]{1,0:T(8,128)(2,1)S(1)}, u32[]{:S(2)}, u32[]{:S(2)}) %collective-permute-start.1) | collective-permute-done | bytes 282656 | tf_op jit(solution)/shard_map/ppermute | solution.py:733
  23.0 4.4 %collective-permute-done.4.refs_8_.refs_13_ = bf16[48,2944]{1,0:T(8,128)(2,1)S(1)} collective-permute-done((bf16[48,2944]{1,0:T(8,128)(2,1)S(1)}, bf16[48,2944]{1,0:T(8,128)(2,1)S(1)}, u32[]{:S(2)}, u32[]{:S(2)}) %collective-permute-start.4) | collective-permute-done | bytes 282656 | tf_op jit(solution)/shard_map/ppermute | solution.py:733
  43.7 21.6 %attn_fwd.2 = (f32[8,1152]{1,0:T(8,128)}, f32[8,256,384]{2,1,0:T(8,128)}, bf16[8,256,1152]{2,1,0:T(8,128)(2,1)}, f32[8,6,256,256]{3,2,1,0:T(8,128)}, bf16[8,256,...) custom-call(bf16[8,384]{1,0:T(8,128)(2,1)} %multiply_convert_fusion.refs_0_, f32[1,11520]{1,0:T(1,128)} %sum_bias.1.refs_1_, ...), custom_call_target="tpu_custom_call" | custom-call | flops 20000000000 | bytes 20000000 | tf_op jit(solution)/shard_map/attn_fwd/pallas_call | solution.py:478
  69.9 4.5 %collective-permute-done.12.refs_8_.refs_13_ = bf16[48,4224]{1,0:T(8,128)(2,1)S(1)} collective-permute-done((bf16[48,4224]{1,0:T(8,128)(2,1)}, bf16[48,4224]{1,0:T(8,128)(2,1)S(1)}, u32[]{:S(2)}, u32[]{:S(2)}) %collective-permute-start.12) | collective-permute-done | bytes 405536 | tf_op jit(solution)/shard_map/ppermute | solution.py:733
  74.4 4.3 %collective-permute-done.14.refs_10_.refs_15_ = bf16[48,4224]{1,0:T(8,128)(2,1)S(1)} collective-permute-done((bf16[48,4224]{1,0:T(8,128)(2,1)S(1)}, bf16[48,4224]{1,0:T(8,128)(2,1)S(1)}, u32[]{:S(2)}, u32[]{:S(2)}) %collective-permute-start.14) | collective-permute-done | bytes 405536 | tf_op jit(solution)/shard_map/ppermute | solution.py:733
  85.2 24.2 %mlp_fwd.2 = (f32[8,1152]{1,0:T(8,128)}, f32[8,256,384]{2,1,0:T(8,128)}, bf16[8,256,384]{2,1,0:T(8,128)(2,1)}, bf16[8,256,1536]{2,1,0:T(8,128)(2,1)}, f32[8,256,1536]{2,1,0:T(8,128)}, /*index=5*/f32[8,256,384]{2,1,0:T(8,128)}) custom-call(bf16[8,384]{1,0:T(8,128)(2,1)} %multiply_convert_fusion.refs_0_, f32[1,11520]{1,0:T(1,128)} %sum_bias.1.refs_1_, ...), custom_call_target="tpu_custom_call" | custom-call | flops 22000001024 | bytes 22000000 | tf_op jit(solution)/shard_map/mlp_fwd/pallas_call | solution.py:478
  114.0 10.1 %collective-permute-done.20.refs_8_.refs_13_ = bf16[48,6912]{1,0:T(8,128)(2,1)S(1)} collective-permute-done((bf16[48,6912]{1,0:T(8,128)(2,1)S(1)}, bf16[48,6912]{1,0:T(8,128)(2,1)S(1)}, u32[]{:S(2)}, u32[]{:S(2)}) %collective-permute-start.20) | collective-permute-done | bytes 663584 | tf_op jit(solution)/shard_map/ppermute | solution.py:733
  124.1 7.1 %collective-permute-done.22.refs_10_.refs_15_ = bf16[48,6912]{1,0:T(8,128)(2,1)S(1)} collective-permute-done((bf16[48,6912]{1,0:T(8,128)(2,1)S(1)}, bf16[48,6912]{1,0:T(8,128)(2,1)S(1)}, u32[]{:S(2)}, u32[]{:S(2)}) %collective-permute-start.22) | collective-permute-done | bytes 663584 | tf_op jit(solution)/shard_map/ppermute | solution.py:733
  135.4 21.6 %attn_fwd.3 = (f32[8,1152]{1,0:T(8,128)}, f32[8,256,384]{2,1,0:T(8,128)}, bf16[8,256,1152]{2,1,0:T(8,128)(2,1)}, f32[8,6,256,256]{3,2,1,0:T(8,128)}, bf16[8,256,...) custom-call(bf16[8,384]{1,0:T(8,128)(2,1)} %multiply_convert_fusion.refs_0_, f32[1,11520]{1,0:T(1,128)} %sum_bias.1.refs_1_, ...), custom_call_target="tpu_custom_call" | custom-call | flops 20000000000 | bytes 20000000 | tf_op jit(solution)/shard_map/attn_fwd/pallas_call | solution.py:478
  157.0 24.2 %mlp_fwd.3 = (f32[8,1152]{1,0:T(8,128)}, f32[8,256,384]{2,1,0:T(8,128)}, bf16[8,256,384]{2,1,0:T(8,128)(2,1)}, bf16[8,256,1536]{2,1,0:T(8,128)(2,1)}, f32[8,256,1536]{2,1,0:T(8,128)}, /*index=5*/f32[8,256,384]{2,1,0:T(8,128)}) custom-call(bf16[8,384]{1,0:T(8,128)(2,1)} %multiply_convert_fusion.refs_0_, f32[1,11520]{1,0:T(1,128)} %sum_bias.1.refs_1_, ...), custom_call_target="tpu_custom_call" | custom-call | flops 22000001024 | bytes 22000000 | tf_op jit(solution)/shard_map/mlp_fwd/pallas_call | solution.py:478
  181.2 25.8 %mlp_bwd.2 = (f32[8,384]{1,0:T(8,128)}, bf16[8,48,2176]{2,1,0:T(8,128)(2,1)}, bf16[8,48,2176]{2,1,0:T(8,128)(2,1)}, f32[8,256,384]{2,1,0:T(8,128)}) custom-call(bf16[8,384]{1,0:T(8,128)(2,1)} %multiply_convert_fusion.refs_0_, f32[8,1152]{1,0:T(8,128)} %get-tuple-element.156.refs_1_, f32[8,256,384]{2,1,0:T(8,128)} %get-tuple-element.151.refs_2_, ...), custom_call_target="tpu_custom_call" | custom-call | flops 24000000000 | bytes 24000000 | tf_op jit(solution)/shard_map/mlp_bwd/pallas_call | solution.py:478
  207.0 3.7 collective-permute-done.24.r_ref
  212.0 3.3 add_split.8
  217.0 29.2 %attn_bwd.2 = (f32[8,384]{1,0:T(8,128)}, bf16[8,48,1408]{2,1,0:T(8,128)(2,1)}, bf16[8,48,1408]{2,1,0:T(8,128)(2,1)}, f32[8,256,384]{2,1,0:T(8,128)}) custom-call(bf16[8,384]{1,0:T(8,128)(2,1)} %multiply_convert_fusion.refs_0_, f32[8,1152]{1,0:T(8,128)} %get-tuple-element.155.refs_1_, f32[8,256,384]{2,1,0:T(8,128)} %get-tuple-element.148.refs_2_, ...), custom_call_target="tpu_custom_call" | custom-call | flops 28000000000 | bytes 28000000 | tf_op jit(solution)/shard_map/attn_bwd/pallas_call | solution.py:478
  258.0 25.7 %mlp_bwd.3 = (f32[8,384]{1,0:T(8,128)}, bf16[8,48,2176]{2,1,0:T(8,128)(2,1)}, bf16[8,48,2176]{2,1,0:T(8,128)(2,1)}, f32[8,256,384]{2,1,0:T(8,128)}) custom-call(bf16[8,384]{1,0:T(8,128)(2,1)} %multiply_convert_fusion.refs_0_, f32[8,1152]{1,0:T(8,128)} %get-tuple-element.154.refs_1_, f32[8,256,384]{2,1,0:T(8,128)} %get-tuple-element.143.refs_2_, ...), custom_call_target="tpu_custom_call" | custom-call | flops 24000000000 | bytes 24000000 | tf_op jit(solution)/shard_map/mlp_bwd/pallas_call | solution.py:478
  290.1 3.8 collective-permute-start.34
  295.7 3.3 add_split.12
  300.6 29.2 %attn_bwd.3 = (f32[8,384]{1,0:T(8,128)}, bf16[8,48,1408]{2,1,0:T(8,128)(2,1)}, bf16[8,48,1408]{2,1,0:T(8,128)(2,1)}, f32[8,256,384]{2,1,0:T(8,128)}) custom-call(bf16[8,384]{1,0:T(8,128)(2,1)} %multiply_convert_fusion.refs_0_, f32[8,1152]{1,0:T(8,128)} %get-tuple-element.153.refs_1_, f32[8,256,384]{2,1,0:T(8,128)} %refs_2_.3, ...), custom_call_target="tpu_custom_call" | custom-call | flops 28000000000 | bytes 28000000 | tf_op jit(solution)/shard_map/attn_bwd/pallas_call | solution.py:478
  339.5 3.8 collective-permute-start.45
  346.2 4.9 %collective-permute-done.38.r_ref = bf16[4,48,1408]{2,1,0:T(8,128)(2,1)S(1)} collective-permute-done((bf16[4,48,1408]{2,1,0:T(8,128)(2,1)}, bf16[4,48,1408]{2,1,0:T(8,128)(2,1)S(1)}, u32[]{:S(2)}, u32[]{:S(2)}) %collective-permute-start.38) | collective-permute-done | bytes 540704 | tf_op jit(solution)/shard_map/ppermute | solution.py:733
  353.9 3.8 collective-permute-start.40
  365.8 5.8 %collective-permute-done.40.refs_2_ = bf16[1,48,1408]{2,1,0:T(8,128)(2,1)S(1)} collective-permute-done((bf16[1,48,1408]{2,1,0:T(8,128)(2,1)}, bf16[1,48,1408]{2,1,0:T(8,128)(2,1)S(1)}, u32[]{:S(2)}, u32[]{:S(2)}) %collective-permute-start.40) | collective-permute-done | bytes 135200 | tf_op jit(solution)/shard_map/ppermute | solution.py:733
  384.5 3.2 unpack.1
  (230 shorter events, 106.2 us)
Async XLA Ops:
  22.4 15.6 %collective-permute-start.2 = (bf16[48,2944]{1,0:T(8,128)(2,1)S(1)}, bf16[48,2944]{1,0:T(8,128)(2,1)S(1)}, u32[]{:S(2)}, u32[]{:S(2)}) collective-permute-start(bf16[48,2944]{1,0:T(8,128)(2,1)S(1)} %collective-permute-done.refs_4_.refs_9_), channel_id=1, source_target_pairs={{0,1},{1,0},{2,3},{3,2},{4,5},{5,4},{6,7},{7,6},{8,9},{9,8},{10,11... | collective-permute-start | bytes 847880 | tf_op jit(solution)/shard_map/ppermute | solution.py:733
  22.5 17.6 %collective-permute-start.3 = (bf16[48,2944]{1,0:T(8,128)(2,1)S(1)}, bf16[48,2944]{1,0:T(8,128)(2,1)S(1)}, u32[]{:S(2)}, u32[]{:S(2)}) collective-permute-start(bf16[48,2944]{1,0:T(8,128)(2,1)S(1)} %collective-permute-done.1.refs_5_.refs_10_), channel_id=1, source_target_pairs={{0,1},{1,0},{2,3},{3,2},{4,5},{5,4},{6,7},{7,6},{8,9},{9,8},{10,11... | collective-permute-start | bytes 847880 | tf_op jit(solution)/shard_map/ppermute | solution.py:733
  35.6 29.7 %collective-permute-start.9 = (bf16[48,4224]{1,0:T(8,128)(2,1)}, bf16[48,4224]{1,0:T(8,128)(2,1)S(1)}, u32[]{:S(2)}, u32[]{:S(2)}) collective-permute-start(bf16[48,4224]{1,0:T(8,128)(2,1)} %get-tuple-element.142.refs_3_.refs_8_), channel_id=1, source_target_pairs={{0,24},{1,5},{2,26},{3,7},{4,28},{5,1},{6,30},{7,3},{8,16},{9,13},... | collective-permute-start | bytes 1216520 | tf_op jit(solution)/shard_map/ppermute | solution.py:733
  38.0 27.3 %collective-permute-start.8 = (bf16[48,4224]{1,0:T(8,128)(2,1)}, bf16[48,4224]{1,0:T(8,128)(2,1)}, u32[]{:S(2)}, u32[]{:S(2)}) collective-permute-start(bf16[48,4224]{1,0:T(8,128)(2,1)} %get-tuple-element.142.refs_3_.refs_8_), channel_id=1, source_target_pairs={{0,8},{1,17},{2,10},{3,19},{4,12},{5,21},{6,14},{7,23},{8,0},{9,25... | collective-permute-start | bytes 1216520 | tf_op jit(solution)/shard_map/ppermute | solution.py:733
  80.8 28.5 %collective-permute-start.17 = (bf16[48,6912]{1,0:T(8,128)(2,1)S(1)}, bf16[48,6912]{1,0:T(8,128)(2,1)S(1)}, u32[]{:S(2)}, u32[]{:S(2)}) collective-permute-start(bf16[48,6912]{1,0:T(8,128)(2,1)S(1)} %copy-done.20), channel_id=1, source_target_pairs={{0,24},{1,5},{2,26},{3,7},{4,28},{5,1},{6,30},{7,3},{8,16},{9,13},... | collective-permute-start | bytes 1990664 | tf_op jit(solution)/shard_map/ppermute | solution.py:733
  83.6 25.8 %collective-permute-start.16 = (bf16[48,6912]{1,0:T(8,128)(2,1)S(1)}, bf16[48,6912]{1,0:T(8,128)(2,1)S(1)}, u32[]{:S(2)}, u32[]{:S(2)}) collective-permute-start(bf16[48,6912]{1,0:T(8,128)(2,1)S(1)} %copy-done.20), channel_id=1, source_target_pairs={{0,8},{1,17},{2,10},{3,19},{4,12},{5,21},{6,14},{7,23},{8,0},{9,25... | collective-permute-start | bytes 1990664 | tf_op jit(solution)/shard_map/ppermute | solution.py:733
  110.5 20.7 %collective-permute-start.22 = (bf16[48,6912]{1,0:T(8,128)(2,1)S(1)}, bf16[48,6912]{1,0:T(8,128)(2,1)S(1)}, u32[]{:S(2)}, u32[]{:S(2)}) collective-permute-start(bf16[48,6912]{1,0:T(8,128)(2,1)S(1)} %collective-permute-done.17.refs_5_.refs_10_), channel_id=1, source_target_pairs={{0,4},{2,6},{4,0},{6,2},{8,12},{10,14},{12,8},{14,10},{16,20},{18,... | collective-permute-start | bytes 1990664 | tf_op jit(solution)/shard_map/ppermute | solution.py:733
  113.4 19.9 %collective-permute-start.18 = (bf16[48,6912]{1,0:T(8,128)(2,1)S(1)}, bf16[48,6912]{1,0:T(8,128)(2,1)S(1)}, u32[]{:S(2)}, u32[]{:S(2)}) collective-permute-start(bf16[48,6912]{1,0:T(8,128)(2,1)S(1)} %collective-permute-done.16.refs_4_.refs_9_), channel_id=1, source_target_pairs={{0,1},{1,0},{2,3},{3,2},{4,5},{5,4},{6,7},{7,6},{8,9},{9,8},{10,11... | collective-permute-start | bytes 1990664 | tf_op jit(solution)/shard_map/ppermute | solution.py:733
  113.5 19.9 %collective-permute-start.19 = (bf16[48,6912]{1,0:T(8,128)(2,1)S(1)}, bf16[48,6912]{1,0:T(8,128)(2,1)S(1)}, u32[]{:S(2)}, u32[]{:S(2)}) collective-permute-start(bf16[48,6912]{1,0:T(8,128)(2,1)S(1)} %collective-permute-done.17.refs_5_.refs_10_), channel_id=1, source_target_pairs={{0,1},{1,0},{2,3},{3,2},{4,5},{5,4},{6,7},{7,6},{8,9},{9,8},{10,11... | collective-permute-start | bytes 1990664 | tf_op jit(solution)/shard_map/ppermute | solution.py:733
  215.3 30.9 %collective-permute-start.25 = (bf16[4,48,2176]{2,1,0:T(8,128)(2,1)}, bf16[4,48,2176]{2,1,0:T(8,128)(2,1)S(1)}, u32[]{:S(2)}, u32[]{:S(2)}) collective-permute-start(bf16[4,48,2176]{2,1,0:T(8,128)(2,1)} %get-tuple-element.176), channel_id=1, source_target_pairs={{0,4},{1,5},{2,6},{3,7},{4,0},{5,1},{6,2},{7,3},{8,12},{9,13},{10,... | collective-permute-start | bytes 2506760 | tf_op jit(solution)/shard_map/ppermute | solution.py:733
  249.5 34.2 %collective-permute-start.27 = (bf16[1,48,2176]{2,1,0:T(8,128)(2,1)}, bf16[1,48,2176]{2,1,0:T(8,128)(2,1)S(1)}, u32[]{:S(2)}, u32[]{:S(2)}) collective-permute-start(bf16[1,48,2176]{2,1,0:T(8,128)(2,1)} %get-tuple-element.191), channel_id=1, source_target_pairs={{0,8},{1,9},{2,10},{3,11},{4,12},{5,13},{6,14},{7,15},{8,0},{9,1},... | collective-permute-start | bytes 626696 | tf_op jit(solution)/shard_map/ppermute | solution.py:733
  250.2 33.5 %collective-permute-start.28 = (bf16[1,48,2176]{2,1,0:T(8,128)(2,1)}, bf16[1,48,2176]{2,1,0:T(8,128)(2,1)S(1)}, u32[]{:S(2)}, u32[]{:S(2)}) collective-permute-start(bf16[1,48,2176]{2,1,0:T(8,128)(2,1)} %get-tuple-element.192), channel_id=1, source_target_pairs={{0,16},{1,17},{2,18},{3,19},{4,20},{5,21},{6,22},{7,23},{8,24},{9,... | collective-permute-start | bytes 626696 | tf_op jit(solution)/shard_map/ppermute | solution.py:733
  253.3 30.4 %collective-permute-start.29 = (bf16[1,48,2176]{2,1,0:T(8,128)(2,1)}, bf16[1,48,2176]{2,1,0:T(8,128)(2,1)S(1)}, u32[]{:S(2)}, u32[]{:S(2)}) collective-permute-start(bf16[1,48,2176]{2,1,0:T(8,128)(2,1)} %get-tuple-element.193), channel_id=1, source_target_pairs={{0,24},{1,25},{2,26},{3,27},{4,28},{5,29},{6,30},{7,31},{8,16},{9,... | collective-permute-start | bytes 626696 | tf_op jit(solution)/shard_map/ppermute | solution.py:733
  257.5 26.3 %collective-permute-start.30 = (bf16[4,48,1408]{2,1,0:T(8,128)(2,1)}, bf16[4,48,1408]{2,1,0:T(8,128)(2,1)S(1)}, u32[]{:S(2)}, u32[]{:S(2)}) collective-permute-start(bf16[4,48,1408]{2,1,0:T(8,128)(2,1)} %get-tuple-element.196), channel_id=1, source_target_pairs={{0,4},{1,5},{2,6},{3,7},{4,0},{5,1},{6,2},{7,3},{8,12},{9,13},{10,... | collective-permute-start | bytes 1622024 | tf_op jit(solution)/shard_map/ppermute | solution.py:733
  286.6 43.3 %collective-permute-start.32 = (bf16[1,48,2176]{2,1,0:T(8,128)(2,1)}, bf16[1,48,2176]{2,1,0:T(8,128)(2,1)S(1)}, u32[]{:S(2)}, u32[]{:S(2)}) collective-permute-start(bf16[1,48,2176]{2,1,0:T(8,128)(2,1)} %add_all.8.refs_0_), channel_id=1, source_target_pairs={{0,2},{1,3},{2,0},{3,1},{4,6},{5,7},{6,4},{7,5},{8,10},{9,11},{10,... | collective-permute-start | bytes 626696 | tf_op jit(solution)/shard_map/ppermute | solution.py:733
  290.1 39.7 %collective-permute-start.33 = (bf16[1,48,1408]{2,1,0:T(8,128)(2,1)}, bf16[1,48,1408]{2,1,0:T(8,128)(2,1)S(1)}, u32[]{:S(2)}, u32[]{:S(2)}) collective-permute-start(bf16[1,48,1408]{2,1,0:T(8,128)(2,1)} %get-tuple-element.215), channel_id=1, source_target_pairs={{0,8},{1,9},{2,10},{3,11},{4,12},{5,13},{6,14},{7,15},{8,0},{9,1},... | collective-permute-start | bytes 405512 | tf_op jit(solution)/shard_map/ppermute | solution.py:733
  290.1 39.7 %collective-permute-start.34 = (bf16[1,48,1408]{2,1,0:T(8,128)(2,1)}, bf16[1,48,1408]{2,1,0:T(8,128)(2,1)S(1)}, u32[]{:S(2)}, u32[]{:S(2)}) collective-permute-start(bf16[1,48,1408]{2,1,0:T(8,128)(2,1)} %get-tuple-element.216), channel_id=1, source_target_pairs={{0,16},{1,17},{2,18},{3,19},{4,20},{5,21},{6,22},{7,23},{8,24},{9,... | collective-permute-start | bytes 405512 | tf_op jit(solution)/shard_map/ppermute | solution.py:733
  293.9 35.9 %collective-permute-start.35 = (bf16[1,48,1408]{2,1,0:T(8,128)(2,1)}, bf16[1,48,1408]{2,1,0:T(8,128)(2,1)S(1)}, u32[]{:S(2)}, u32[]{:S(2)}) collective-permute-start(bf16[1,48,1408]{2,1,0:T(8,128)(2,1)} %get-tuple-element.217), channel_id=1, source_target_pairs={{0,24},{1,25},{2,26},{3,27},{4,28},{5,29},{6,30},{7,31},{8,16},{9,... | collective-permute-start | bytes 405512 | tf_op jit(solution)/shard_map/ppermute | solution.py:733
  299.0 30.8 %collective-permute-start.36 = (bf16[4,48,2176]{2,1,0:T(8,128)(2,1)}, bf16[4,48,2176]{2,1,0:T(8,128)(2,1)S(1)}, u32[]{:S(2)}, u32[]{:S(2)}) collective-permute-start(bf16[4,48,2176]{2,1,0:T(8,128)(2,1)} %get-tuple-element.220), channel_id=1, source_target_pairs={{0,4},{1,5},{2,6},{3,7},{4,0},{5,1},{6,2},{7,3},{8,12},{9,13},{10,... | collective-permute-start | bytes 2506760 | tf_op jit(solution)/shard_map/ppermute | solution.py:733
  339.5 19.0 %collective-permute-start.45 = (bf16[1,48,2176]{2,1,0:T(8,128)(2,1)}, bf16[1,48,2176]{2,1,0:T(8,128)(2,1)S(1)}, u32[]{:S(2)}, u32[]{:S(2)}) collective-permute-start(bf16[1,48,2176]{2,1,0:T(8,128)(2,1)} %get-tuple-element.241), channel_id=1, source_target_pairs={{0,16},{1,17},{2,18},{3,19},{4,20},{5,21},{6,22},{7,23},{8,24},{9,... | collective-permute-start | bytes 626696 | tf_op jit(solution)/shard_map/ppermute | solution.py:733
  343.3 17.5 %collective-permute-start.46 = (bf16[1,48,2176]{2,1,0:T(8,128)(2,1)}, bf16[1,48,2176]{2,1,0:T(8,128)(2,1)S(1)}, u32[]{:S(2)}, u32[]{:S(2)}) collective-permute-start(bf16[1,48,2176]{2,1,0:T(8,128)(2,1)} %get-tuple-element.242), channel_id=1, source_target_pairs={{0,24},{1,25},{2,26},{3,27},{4,28},{5,29},{6,30},{7,31},{8,16},{9,... | collective-permute-start | bytes 626696 | tf_op jit(solution)/shard_map/ppermute | solution.py:733
  345.7 29.0 %collective-permute-start.49 = (bf16[1,48,1408]{2,1,0:T(8,128)(2,1)}, bf16[1,48,1408]{2,1,0:T(8,128)(2,1)S(1)}, u32[]{:S(2)}, u32[]{:S(2)}) collective-permute-start(bf16[1,48,1408]{2,1,0:T(8,128)(2,1)} %add_all.13.refs_0_), channel_id=1, source_target_pairs={{0,2},{1,3},{2,0},{3,1},{4,6},{5,7},{6,4},{7,5},{8,10},{9,11},{10,... | collective-permute-start | bytes 405512 | tf_op jit(solution)/shard_map/ppermute | solution.py:733
  353.9 17.7 %collective-permute-start.40 = (bf16[1,48,1408]{2,1,0:T(8,128)(2,1)}, bf16[1,48,1408]{2,1,0:T(8,128)(2,1)S(1)}, u32[]{:S(2)}, u32[]{:S(2)}) collective-permute-start(bf16[1,48,1408]{2,1,0:T(8,128)(2,1)} %get-tuple-element.235), channel_id=1, source_target_pairs={{0,16},{1,17},{2,18},{3,19},{4,20},{5,21},{6,22},{7,23},{8,24},{9,... | collective-permute-start | bytes 405512 | tf_op jit(solution)/shard_map/ppermute | solution.py:733
  365.8 17.2 %collective-permute-start.51 = (bf16[1,48,2176]{2,1,0:T(8,128)(2,1)}, bf16[1,48,2176]{2,1,0:T(8,128)(2,1)S(1)}, u32[]{:S(2)}, u32[]{:S(2)}) collective-permute-start(bf16[1,48,2176]{2,1,0:T(8,128)(2,1)} %add_all.15), channel_id=1, source_target_pairs={{0,1},{1,0},{2,3},{3,2},{4,5},{5,4},{6,7},{7,6},{8,9},{9,8},{10,11... | collective-permute-start | bytes 626696 | tf_op jit(solution)/shard_map/ppermute | solution.py:733
  (84 other events, 691.6 us)
